TPU v7x, 32 devices: a whole 2x2x4 slice. The times are simulated.
32 devices in a mesh: state: 4 (over y, x), space: 8 (over z, core).
Axes of the slice: x: 2, y: 2, z: 4, core: 2. Of those that a mesh axis runs over, the one named last changes fastest.
Arguments:
- states_in: bfloat16 [384, 8192], P('state', 'space'), may hold values from -12 to 12
- cell_matrices: bfloat16 [16, 512, 512], P('space'), may hold values from -0.5 to 1.5, as said below
- connectivity: int32 [16, 512], P('space'), may hold values from 0 to 8191, as said below
- potential: float32 [8192], P('space'), may hold values from 0.2 to 1.2
Outputs:
- filtered: bfloat16 [384, 8192], P('state', 'space')
- intersection: float32 [384, 384], P('state', 'space')
- projected: float32 [384, 384], P('state', 'space')
Inputs may be any that keep to these rules, and one draw needn't show every extreme that they name: `cell_matrices`: each cell's matrix is symmetric. `connectivity`: the cells of rows s * 2 to (s + 1) * 2 - 1 name only nodes from s * 1024 - 128 to (s + 1) * 1024 + 127. A node may be named by several cells, or twice in one cell, or by none.
All inputs are finite; a program needn't handle non-finite values.
Results may differ from a plain program's by a relative error of at most 0.019.
Values may be sent and summed in bfloat16 or wider, within the bound.
No kernel may reach another device: no remote copies, remote signals or barrier semaphores. Data moves between devices by JAX's collectives and lax.ppermute only.
A program may use at most 64 MiB of HBM per device.

v0:
```python
import jax
import jax.numpy as jnp
from jax import lax
from jax.sharding import PartitionSpec as P

DEGREE = 4


spectrum_center = 3.0
spectrum_half = 3.5


def padded(shard, sides, width):
    for axis, dim in sides:
        size, length = (lax.axis_size(axis), shard.shape[dim])
        up = [(i, (i + 1) % size) for i in range(size - 1)]
        down = [(j, i) for i, j in up]
        last = lax.slice_in_dim(shard, length - width, length, axis=dim)
        leading = lax.slice_in_dim(shard, 0, width, axis=dim)
        before = lax.ppermute(last, axis, up)
        after = lax.ppermute(leading, axis, down)
        shard = jnp.concatenate([before, shard, after], axis=dim)
    return shard


def shifted(block, axis, distance):
    devices = range(lax.axis_size(axis))
    route = [(i - distance, i) for i in devices if i - distance in devices]
    return lax.ppermute(block, axis, route)


def apply_hamiltonian(states, cell_matrices, local_index, potential, rim_width):
    node_count = states.shape[1]
    extended = padded(states, (("space", 1),), rim_width)
    picked = extended[:, local_index]
    products = jnp.einsum("scp,cpq->scq", picked, cell_matrices, preferred_element_type=jnp.float32)
    summed = jnp.zeros(extended.shape, jnp.float32)
    summed = summed.at[:, local_index.reshape(-1)].add(products.reshape(states.shape[0], -1))
    owned = summed[:, rim_width : rim_width + node_count]
    from_upper = shifted(summed[:, :rim_width], "space", -1)
    from_lower = shifted(summed[:, rim_width + node_count :], "space", 1)
    owned = owned.at[:, node_count - rim_width :].add(from_upper)
    owned = owned.at[:, :rim_width].add(from_lower)
    return owned + potential[None, :] * states.astype(jnp.float32)


def per_device(states_in, cell_matrices, connectivity, potential):
    node_count = states_in.shape[1]
    rim_width = cell_matrices.shape[1] // 4
    offset = lax.axis_index("space") * node_count - rim_width
    local_index = connectivity - offset
    earlier = states_in
    first = (
        apply_hamiltonian(earlier, cell_matrices, local_index, potential, rim_width)
        - spectrum_center * earlier.astype(jnp.float32)
    ) / spectrum_half
    current = first.astype(jnp.bfloat16)
    for section_index in range(DEGREE - 1):
        image = apply_hamiltonian(current, cell_matrices, local_index, potential, rim_width)
        following = 2.0 * (
            image - spectrum_center * current.astype(jnp.float32)
        ) / spectrum_half - earlier.astype(jnp.float32)
        earlier = current
        current = following.astype(jnp.bfloat16)
    total_nodes = node_count * lax.axis_size("space")
    contract = (((1,), (1,)), ((), ()))
    energy = apply_hamiltonian(current, cell_matrices, local_index, potential, rim_width)
    incoming = lax.all_gather(current, "state", axis=0, tiled=True)
    block_intersection = lax.dot_general(
        current, incoming, contract, preferred_element_type=jnp.float32
    )
    block_energy = lax.dot_general(
        energy, incoming.astype(jnp.float32), contract, precision=lax.Precision.HIGHEST
    )
    intersection = block_intersection
    projected = block_energy
    intersection = intersection / total_nodes
    projected = projected / total_nodes
    intersection, projected = (
        lax.psum_scatter(
            intersection.astype(jnp.bfloat16), "space", scatter_dimension=1, tiled=True
        ).astype(jnp.float32),
        lax.psum_scatter(
            projected.astype(jnp.bfloat16), "space", scatter_dimension=1, tiled=True
        ).astype(jnp.float32),
    )
    return (current, intersection, projected)


def solution(mesh):
    return jax.shard_map(
        per_device,
        mesh=mesh,
        in_specs=(P("state", "space"), P("space", None, None), P("space", None), P("space")),
        out_specs=(P("state", "space"), P("state", "space"), P("state", "space")),
        check_vma=False,
    )
```

profile of v0, /device:TPU:0, one launch (start us, length us, event | category | flops | bytes accessed | tf_op | source)
XLA Modules:
  0.0 222.2 jit_solution(10412966935368874922)
XLA Ops:
  12.9 3.2 %collective-permute-done.1 = bf16[96,128]{0,1:T(8,128)(2,1)S(1)} collective-permute-done((bf16[96,128]{0,1:T(8,128)(2,1)S(1)}, bf16[96,128]{0,1:T(8,128)(2,1)S(1)}, u32[]{:S(2)}, u32[]{:S(2)}) %collective-permute-start.1) | collective-permute-done | bytes 24608 | tf_op jit(solution)/shard_map/ppermute | solution.py:21
  16.2 3.2 %gather_fusion = bf16[1024,96]{1,0:T(8,128)(2,1)S(1)} fusion(bf16[96,1280]{0,1:T(8,128)(2,1)S(1)} %pad_maximum_fusion, s32[1024]{0:T(1024)S(1)} %broadcast_clamp_fusion), kind=kCustom, calls=%fused_computation | custom fusion | bytes 397312 | tf_op jit(solution)/shard_map/gather | solution.py:35
  20.1 6.2 %scatter_custom_fusion = f32[96,1280]{0,1:T(8,128)S(1)} fusion(s32[1024]{0:T(1024)S(1)} %bitcast.79, f32[1024,96]{1,0:T(8,128)S(1)} %copy.42, f32[]{:T(128)} %constant.237.clone.1), kind=kCustom, calls=%fused_computation.62 | custom fusion | flops 98304 | bytes 491524 | tf_op jit(solution)/shard_map/scatter-add | solution.py:38
  28.3 5.2 %collective-permute-start.3 = (f32[96,128]{0,1:T(8,128)S(1)}, f32[96,128]{0,1:T(8,128)S(1)}, u32[]{:S(2)}, u32[]{:S(2)}) collective-permute-start(f32[96,128]{0,1:T(8,128)S(1)} %get-tuple-element.140), channel_id=1, source_target_pairs={{0,1},{1,2},{2,3},{3,4},{4,5},{5,6},{6,7},{8,9},{9,10},{10,11},{11... | collective-permute-start | bytes 147464 | tf_op jit(solution)/shard_map/ppermute | solution.py:29
  35.2 4.1 %collective-permute-start.4 = (bf16[96,128]{0,1:T(8,128)(2,1)S(1)}, bf16[96,128]{0,1:T(8,128)(2,1)S(1)}, u32[]{:S(2)}, u32[]{:S(2)}) collective-permute-start(bf16[96,128]{0,1:T(8,128)(2,1)S(1)} %get-tuple-element.148), channel_id=1, source_target_pairs={{0,1},{1,2},{2,3},{3,4},{4,5},{5,6},{6,7},{8,9},{9,10},{10,11},{11... | collective-permute-start | bytes 73736 | tf_op jit(solution)/shard_map/ppermute | solution.py:20
  40.6 3.7 %collective-permute-done.5 = bf16[96,128]{0,1:T(8,128)(2,1)S(1)} collective-permute-done((bf16[96,128]{0,1:T(8,128)(2,1)S(1)}, bf16[96,128]{0,1:T(8,128)(2,1)S(1)}, u32[]{:S(2)}, u32[]{:S(2)}) %collective-permute-start.5) | collective-permute-done | bytes 24608 | tf_op jit(solution)/shard_map/ppermute | solution.py:21
  44.4 3.2 %gather_fusion.1 = bf16[1024,96]{1,0:T(8,128)(2,1)S(1)} fusion(bf16[96,1280]{0,1:T(8,128)(2,1)S(1)} %pad_maximum_fusion.1, s32[1024]{0:T(1024)S(1)} %broadcast_clamp_fusion), kind=kCustom, calls=%fused_computation.1 | custom fusion | bytes 397312 | tf_op jit(solution)/shard_map/gather | solution.py:35
  48.3 6.2 %scatter_custom_fusion.1 = f32[96,1280]{0,1:T(8,128)S(1)} fusion(s32[1024]{0:T(1024)S(1)} %bitcast.80, f32[1024,96]{1,0:T(8,128)S(1)} %copy.46, f32[]{:T(128)} %constant.237.clone.1), kind=kCustom, calls=%fused_computation.60 | custom fusion | flops 98304 | bytes 491524 | tf_op jit(solution)/shard_map/scatter-add | solution.py:38
  55.8 5.2 %collective-permute-start.7 = (f32[96,128]{0,1:T(8,128)S(1)}, f32[96,128]{0,1:T(8,128)S(1)}, u32[]{:S(2)}, u32[]{:S(2)}) collective-permute-start(f32[96,128]{0,1:T(8,128)S(1)} %get-tuple-element.138), channel_id=1, source_target_pairs={{0,1},{1,2},{2,3},{3,4},{4,5},{5,6},{6,7},{8,9},{9,10},{10,11},{11... | collective-permute-start | bytes 147464 | tf_op jit(solution)/shard_map/ppermute | solution.py:29
  62.8 4.1 %collective-permute-start.8 = (bf16[96,128]{0,1:T(8,128)(2,1)S(1)}, bf16[96,128]{0,1:T(8,128)(2,1)S(1)}, u32[]{:S(2)}, u32[]{:S(2)}) collective-permute-start(bf16[96,128]{0,1:T(8,128)(2,1)S(1)} %get-tuple-element.146), channel_id=1, source_target_pairs={{0,1},{1,2},{2,3},{3,4},{4,5},{5,6},{6,7},{8,9},{9,10},{10,11},{11... | collective-permute-start | bytes 73736 | tf_op jit(solution)/shard_map/ppermute | solution.py:20
  68.2 3.7 %collective-permute-done.9 = bf16[96,128]{0,1:T(8,128)(2,1)S(1)} collective-permute-done((bf16[96,128]{0,1:T(8,128)(2,1)S(1)}, bf16[96,128]{0,1:T(8,128)(2,1)S(1)}, u32[]{:S(2)}, u32[]{:S(2)}) %collective-permute-start.9) | collective-permute-done | bytes 24608 | tf_op jit(solution)/shard_map/ppermute | solution.py:21
  71.9 3.2 %gather_fusion.2 = bf16[1024,96]{1,0:T(8,128)(2,1)S(1)} fusion(bf16[96,1280]{0,1:T(8,128)(2,1)S(1)} %pad_maximum_fusion.2, s32[1024]{0:T(1024)S(1)} %broadcast_clamp_fusion), kind=kCustom, calls=%fused_computation.2 | custom fusion | bytes 397312 | tf_op jit(solution)/shard_map/gather | solution.py:35
  75.8 6.2 %scatter_custom_fusion.2 = f32[96,1280]{0,1:T(8,128)S(1)} fusion(s32[1024]{0:T(1024)S(1)} %bitcast.81, f32[1024,96]{1,0:T(8,128)S(1)} %copy.49, f32[]{:T(128)} %constant.237.clone.1), kind=kCustom, calls=%fused_computation.58 | custom fusion | flops 98304 | bytes 491524 | tf_op jit(solution)/shard_map/scatter-add | solution.py:38
  83.4 5.2 %collective-permute-start.11 = (f32[96,128]{0,1:T(8,128)S(1)}, f32[96,128]{0,1:T(8,128)S(1)}, u32[]{:S(2)}, u32[]{:S(2)}) collective-permute-start(f32[96,128]{0,1:T(8,128)S(1)} %get-tuple-element.136), channel_id=1, source_target_pairs={{0,1},{1,2},{2,3},{3,4},{4,5},{5,6},{6,7},{8,9},{9,10},{10,11},{11... | collective-permute-start | bytes 147464 | tf_op jit(solution)/shard_map/ppermute | solution.py:29
  90.4 4.1 %collective-permute-start.12 = (bf16[96,128]{0,1:T(8,128)(2,1)S(1)}, bf16[96,128]{0,1:T(8,128)(2,1)S(1)}, u32[]{:S(2)}, u32[]{:S(2)}) collective-permute-start(bf16[96,128]{0,1:T(8,128)(2,1)S(1)} %get-tuple-element.144), channel_id=1, source_target_pairs={{0,1},{1,2},{2,3},{3,4},{4,5},{5,6},{6,7},{8,9},{9,10},{10,11},{11... | collective-permute-start | bytes 73736 | tf_op jit(solution)/shard_map/ppermute | solution.py:20
  96.0 3.5 %collective-permute-done.13 = bf16[96,128]{0,1:T(8,128)(2,1)S(1)} collective-permute-done((bf16[96,128]{0,1:T(8,128)(2,1)S(1)}, bf16[96,128]{0,1:T(8,128)(2,1)S(1)}, u32[]{:S(2)}, u32[]{:S(2)}) %collective-permute-start.13) | collective-permute-done | bytes 24608 | tf_op jit(solution)/shard_map/ppermute | solution.py:21
  103.4 6.2 %scatter_custom_fusion.3 = f32[96,1280]{0,1:T(8,128)S(1)} fusion(s32[1024]{0:T(1024)S(1)} %bitcast.82, f32[1024,96]{1,0:T(8,128)S(1)} %copy.52, f32[]{:T(128)} %constant.237.clone.1), kind=kCustom, calls=%fused_computation.56 | custom fusion | flops 98304 | bytes 491524 | tf_op jit(solution)/shard_map/scatter-add | solution.py:38
  111.0 5.2 %collective-permute-start.15 = (f32[96,128]{0,1:T(8,128)S(1)}, f32[96,128]{0,1:T(8,128)S(1)}, u32[]{:S(2)}, u32[]{:S(2)}) collective-permute-start(f32[96,128]{0,1:T(8,128)S(1)} %get-tuple-element.134), channel_id=1, source_target_pairs={{0,1},{1,2},{2,3},{3,4},{4,5},{5,6},{6,7},{8,9},{9,10},{10,11},{11... | collective-permute-start | bytes 147464 | tf_op jit(solution)/shard_map/ppermute | solution.py:29
  118.2 4.1 %collective-permute-start.16 = (bf16[96,128]{0,1:T(8,128)(2,1)S(1)}, bf16[96,128]{0,1:T(8,128)(2,1)S(1)}, u32[]{:S(2)}, u32[]{:S(2)}) collective-permute-start(bf16[96,128]{0,1:T(8,128)(2,1)S(1)} %get-tuple-element.142), channel_id=1, source_target_pairs={{0,1},{1,2},{2,3},{3,4},{4,5},{5,6},{6,7},{8,9},{9,10},{10,11},{11... | collective-permute-start | bytes 73736 | tf_op jit(solution)/shard_map/ppermute | solution.py:20
  123.5 12.1 %all_gather.3 = bf16[384,1024]{1,0:T(8,128)(2,1)S(1)} all-gather(bf16[96,1024]{1,0:T(8,128)(2,1)S(1)} %copy.57), channel_id=1, replica_groups=mesh['state'=4,'space'=8] {'state'}, dimensions={0}, use_global_device_ids=true | all-gather | bytes 983040 | tf_op jit(solution)/shard_map/all_gather | solution.py:68
  139.6 6.2 %scatter_custom_fusion.4 = f32[96,1280]{0,1:T(8,128)S(1)} fusion(s32[1024]{0:T(1024)S(1)} %bitcast.83, f32[1024,96]{1,0:T(8,128)S(1)} %copy.56, f32[]{:T(128)} %constant.237.clone.1), kind=kCustom, calls=%fused_computation.54 | custom fusion | flops 98304 | bytes 491524 | tf_op jit(solution)/shard_map/scatter-add | solution.py:38
  148.3 3.5 %collective-permute-start.19 = (f32[96,128]{0,1:T(8,128)S(1)}, f32[96,128]{0,1:T(8,128)S(1)}, u32[]{:S(2)}, u32[]{:S(2)}) collective-permute-start(f32[96,128]{0,1:T(8,128)S(1)} %get-tuple-element.132), channel_id=1, source_target_pairs={{0,1},{1,2},{2,3},{3,4},{4,5},{5,6},{6,7},{8,9},{9,10},{10,11},{11... | collective-permute-start | bytes 147464 | tf_op jit(solution)/shard_map/ppermute | solution.py:29
  154.9 28.2 %reduce-scatter.3.cloned.1.call-done = bf16[96,48]{0,1:T(8,128)(2,1)} async-done(((bf16[96,384]{0,1:T(8,128)(2,1)}), bf16[96,48]{0,1:T(8,128)(2,1)}) %reduce-scatter.3.cloned.1.call-update) | async-done | bytes 9232 | tf_op jit(solution)/shard_map/reduce_scatter | solution.py:80
  184.4 29.7 %reduce-scatter.5.cloned.1.call-done = bf16[96,48]{0,1:T(8,128)(2,1)} async-done(((bf16[96,384]{0,1:T(8,128)(2,1)}), bf16[96,48]{0,1:T(8,128)(2,1)}) %reduce-scatter.5.cloned.1.call-update) | async-done | bytes 9232 | tf_op jit(solution)/shard_map/reduce_scatter | solution.py:83
  (107 shorter events, 42.5 us)
Async XLA Ops:
  7.2 12.4 %copy-start = (bf16[2,512,512]{2,1,0:T(8,128)(2,1)S(1)}, bf16[2,512,512]{2,1,0:T(8,128)(2,1)}, u32[]{:S(2)}) copy-start(bf16[2,512,512]{2,1,0:T(8,128)(2,1)} %param.25) | copy-start | bytes 3145732
  7.2 175.9 %reduce-scatter.3.cloned.1.call-start = ((), (), s32[]{:S(2)}) async-start(), calls=%async_computation.2 | async-start | bytes 110592 | tf_op jit(solution)/shard_map/reduce_scatter | solution.py:80
  8.4 4.4 %collective-permute-start = (bf16[96,128]{0,1:T(8,128)(2,1)S(1)}, bf16[96,128]{0,1:T(8,128)(2,1)S(1)}, u32[]{:S(2)}, u32[]{:S(2)}) collective-permute-start(bf16[96,128]{0,1:T(8,128)(2,1)S(1)} %get-tuple-element.150), channel_id=1, source_target_pairs={{0,1},{1,2},{2,3},{3,4},{4,5},{5,6},{6,7},{8,9},{9,10},{10,11},{11... | collective-permute-start | bytes 73736 | tf_op jit(solution)/shard_map/ppermute | solution.py:20
  10.8 5.3 %collective-permute-start.1 = (bf16[96,128]{0,1:T(8,128)(2,1)S(1)}, bf16[96,128]{0,1:T(8,128)(2,1)S(1)}, u32[]{:S(2)}, u32[]{:S(2)}) collective-permute-start(bf16[96,128]{0,1:T(8,128)(2,1)S(1)} %get-tuple-element.151), channel_id=1, source_target_pairs={{1,0},{2,1},{3,2},{4,3},{5,4},{6,5},{7,6},{9,8},{10,9},{11,10},{12... | collective-permute-start | bytes 73736 | tf_op jit(solution)/shard_map/ppermute | solution.py:21
  26.3 7.2 %collective-permute-start.2 = (f32[96,128]{0,1:T(8,128)S(1)}, f32[96,128]{0,1:T(8,128)S(1)}, u32[]{:S(2)}, u32[]{:S(2)}) collective-permute-start(f32[96,128]{0,1:T(8,128)S(1)} %get-tuple-element.141), channel_id=1, source_target_pairs={{1,0},{2,1},{3,2},{4,3},{5,4},{6,5},{7,6},{9,8},{10,9},{11,10},{12... | collective-permute-start | bytes 147464 | tf_op jit(solution)/shard_map/ppermute | solution.py:29
  28.3 6.1 %collective-permute-start.3 = (f32[96,128]{0,1:T(8,128)S(1)}, f32[96,128]{0,1:T(8,128)S(1)}, u32[]{:S(2)}, u32[]{:S(2)}) collective-permute-start(f32[96,128]{0,1:T(8,128)S(1)} %get-tuple-element.140), channel_id=1, source_target_pairs={{0,1},{1,2},{2,3},{3,4},{4,5},{5,6},{6,7},{8,9},{9,10},{10,11},{11... | collective-permute-start | bytes 147464 | tf_op jit(solution)/shard_map/ppermute | solution.py:29
  35.2 5.4 %collective-permute-start.4 = (bf16[96,128]{0,1:T(8,128)(2,1)S(1)}, bf16[96,128]{0,1:T(8,128)(2,1)S(1)}, u32[]{:S(2)}, u32[]{:S(2)}) collective-permute-start(bf16[96,128]{0,1:T(8,128)(2,1)S(1)} %get-tuple-element.148), channel_id=1, source_target_pairs={{0,1},{1,2},{2,3},{3,4},{4,5},{5,6},{6,7},{8,9},{9,10},{10,11},{11... | collective-permute-start | bytes 73736 | tf_op jit(solution)/shard_map/ppermute | solution.py:20
  39.3 5.0 %collective-permute-start.5 = (bf16[96,128]{0,1:T(8,128)(2,1)S(1)}, bf16[96,128]{0,1:T(8,128)(2,1)S(1)}, u32[]{:S(2)}, u32[]{:S(2)}) collective-permute-start(bf16[96,128]{0,1:T(8,128)(2,1)S(1)} %get-tuple-element.149), channel_id=1, source_target_pairs={{1,0},{2,1},{3,2},{4,3},{5,4},{6,5},{7,6},{9,8},{10,9},{11,10},{12... | collective-permute-start | bytes 73736 | tf_op jit(solution)/shard_map/ppermute | solution.py:21
  54.5 6.5 %collective-permute-start.6 = (f32[96,128]{0,1:T(8,128)S(1)}, f32[96,128]{0,1:T(8,128)S(1)}, u32[]{:S(2)}, u32[]{:S(2)}) collective-permute-start(f32[96,128]{0,1:T(8,128)S(1)} %get-tuple-element.139), channel_id=1, source_target_pairs={{1,0},{2,1},{3,2},{4,3},{5,4},{6,5},{7,6},{9,8},{10,9},{11,10},{12... | collective-permute-start | bytes 147464 | tf_op jit(solution)/shard_map/ppermute | solution.py:29
  55.8 6.1 %collective-permute-start.7 = (f32[96,128]{0,1:T(8,128)S(1)}, f32[96,128]{0,1:T(8,128)S(1)}, u32[]{:S(2)}, u32[]{:S(2)}) collective-permute-start(f32[96,128]{0,1:T(8,128)S(1)} %get-tuple-element.138), channel_id=1, source_target_pairs={{0,1},{1,2},{2,3},{3,4},{4,5},{5,6},{6,7},{8,9},{9,10},{10,11},{11... | collective-permute-start | bytes 147464 | tf_op jit(solution)/shard_map/ppermute | solution.py:29
  62.8 5.4 %collective-permute-start.8 = (bf16[96,128]{0,1:T(8,128)(2,1)S(1)}, bf16[96,128]{0,1:T(8,128)(2,1)S(1)}, u32[]{:S(2)}, u32[]{:S(2)}) collective-permute-start(bf16[96,128]{0,1:T(8,128)(2,1)S(1)} %get-tuple-element.146), channel_id=1, source_target_pairs={{0,1},{1,2},{2,3},{3,4},{4,5},{5,6},{6,7},{8,9},{9,10},{10,11},{11... | collective-permute-start | bytes 73736 | tf_op jit(solution)/shard_map/ppermute | solution.py:20
  66.9 5.0 %collective-permute-start.9 = (bf16[96,128]{0,1:T(8,128)(2,1)S(1)}, bf16[96,128]{0,1:T(8,128)(2,1)S(1)}, u32[]{:S(2)}, u32[]{:S(2)}) collective-permute-start(bf16[96,128]{0,1:T(8,128)(2,1)S(1)} %get-tuple-element.147), channel_id=1, source_target_pairs={{1,0},{2,1},{3,2},{4,3},{5,4},{6,5},{7,6},{9,8},{10,9},{11,10},{12... | collective-permute-start | bytes 73736 | tf_op jit(solution)/shard_map/ppermute | solution.py:21
  82.1 6.5 %collective-permute-start.10 = (f32[96,128]{0,1:T(8,128)S(1)}, f32[96,128]{0,1:T(8,128)S(1)}, u32[]{:S(2)}, u32[]{:S(2)}) collective-permute-start(f32[96,128]{0,1:T(8,128)S(1)} %get-tuple-element.137), channel_id=1, source_target_pairs={{1,0},{2,1},{3,2},{4,3},{5,4},{6,5},{7,6},{9,8},{10,9},{11,10},{12... | collective-permute-start | bytes 147464 | tf_op jit(solution)/shard_map/ppermute | solution.py:29
  83.4 6.1 %collective-permute-start.11 = (f32[96,128]{0,1:T(8,128)S(1)}, f32[96,128]{0,1:T(8,128)S(1)}, u32[]{:S(2)}, u32[]{:S(2)}) collective-permute-start(f32[96,128]{0,1:T(8,128)S(1)} %get-tuple-element.136), channel_id=1, source_target_pairs={{0,1},{1,2},{2,3},{3,4},{4,5},{5,6},{6,7},{8,9},{9,10},{10,11},{11... | collective-permute-start | bytes 147464 | tf_op jit(solution)/shard_map/ppermute | solution.py:29
  90.4 5.6 %collective-permute-start.12 = (bf16[96,128]{0,1:T(8,128)(2,1)S(1)}, bf16[96,128]{0,1:T(8,128)(2,1)S(1)}, u32[]{:S(2)}, u32[]{:S(2)}) collective-permute-start(bf16[96,128]{0,1:T(8,128)(2,1)S(1)} %get-tuple-element.144), channel_id=1, source_target_pairs={{0,1},{1,2},{2,3},{3,4},{4,5},{5,6},{6,7},{8,9},{9,10},{10,11},{11... | collective-permute-start | bytes 73736 | tf_op jit(solution)/shard_map/ppermute | solution.py:20
  94.5 5.0 %collective-permute-start.13 = (bf16[96,128]{0,1:T(8,128)(2,1)S(1)}, bf16[96,128]{0,1:T(8,128)(2,1)S(1)}, u32[]{:S(2)}, u32[]{:S(2)}) collective-permute-start(bf16[96,128]{0,1:T(8,128)(2,1)S(1)} %get-tuple-element.145), channel_id=1, source_target_pairs={{1,0},{2,1},{3,2},{4,3},{5,4},{6,5},{7,6},{9,8},{10,9},{11,10},{12... | collective-permute-start | bytes 73736 | tf_op jit(solution)/shard_map/ppermute | solution.py:21
  109.6 6.5 %collective-permute-start.14 = (f32[96,128]{0,1:T(8,128)S(1)}, f32[96,128]{0,1:T(8,128)S(1)}, u32[]{:S(2)}, u32[]{:S(2)}) collective-permute-start(f32[96,128]{0,1:T(8,128)S(1)} %get-tuple-element.135), channel_id=1, source_target_pairs={{1,0},{2,1},{3,2},{4,3},{5,4},{6,5},{7,6},{9,8},{10,9},{11,10},{12... | collective-permute-start | bytes 147464 | tf_op jit(solution)/shard_map/ppermute | solution.py:29
  111.0 6.1 %collective-permute-start.15 = (f32[96,128]{0,1:T(8,128)S(1)}, f32[96,128]{0,1:T(8,128)S(1)}, u32[]{:S(2)}, u32[]{:S(2)}) collective-permute-start(f32[96,128]{0,1:T(8,128)S(1)} %get-tuple-element.134), channel_id=1, source_target_pairs={{0,1},{1,2},{2,3},{3,4},{4,5},{5,6},{6,7},{8,9},{9,10},{10,11},{11... | collective-permute-start | bytes 147464 | tf_op jit(solution)/shard_map/ppermute | solution.py:29
  118.2 17.4 %copy-start.1 = (bf16[96,1024]{1,0:T(8,128)(2,1)}, bf16[96,1024]{1,0:T(8,128)(2,1)S(1)}, u32[]{:S(2)}) copy-start(bf16[96,1024]{1,0:T(8,128)(2,1)S(1)} %copy.57) | copy-start | bytes 589828
  118.2 17.4 %collective-permute-start.16 = (bf16[96,128]{0,1:T(8,128)(2,1)S(1)}, bf16[96,128]{0,1:T(8,128)(2,1)S(1)}, u32[]{:S(2)}, u32[]{:S(2)}) collective-permute-start(bf16[96,128]{0,1:T(8,128)(2,1)S(1)} %get-tuple-element.142), channel_id=1, source_target_pairs={{0,1},{1,2},{2,3},{3,4},{4,5},{5,6},{6,7},{8,9},{9,10},{10,11},{11... | collective-permute-start | bytes 73736 | tf_op jit(solution)/shard_map/ppermute | solution.py:20
  122.2 13.4 %collective-permute-start.17 = (bf16[96,128]{0,1:T(8,128)(2,1)S(1)}, bf16[96,128]{0,1:T(8,128)(2,1)S(1)}, u32[]{:S(2)}, u32[]{:S(2)}) collective-permute-start(bf16[96,128]{0,1:T(8,128)(2,1)S(1)} %get-tuple-element.143), channel_id=1, source_target_pairs={{1,0},{2,1},{3,2},{4,3},{5,4},{6,5},{7,6},{9,8},{10,9},{11,10},{12... | collective-permute-start | bytes 73736 | tf_op jit(solution)/shard_map/ppermute | solution.py:21
  145.8 6.0 %collective-permute-start.18 = (f32[96,128]{0,1:T(8,128)S(1)}, f32[96,128]{0,1:T(8,128)S(1)}, u32[]{:S(2)}, u32[]{:S(2)}) collective-permute-start(f32[96,128]{0,1:T(8,128)S(1)} %get-tuple-element.133), channel_id=1, source_target_pairs={{1,0},{2,1},{3,2},{4,3},{5,4},{6,5},{7,6},{9,8},{10,9},{11,10},{12... | collective-permute-start | bytes 147464 | tf_op jit(solution)/shard_map/ppermute | solution.py:29
  148.2 65.9 %reduce-scatter.5.cloned.1.call-start = ((), (), s32[]{:S(2)}) async-start(), calls=%async_computation.3 | async-start | bytes 110592 | tf_op jit(solution)/shard_map/reduce_scatter | solution.py:83
  148.3 4.4 %collective-permute-start.19 = (f32[96,128]{0,1:T(8,128)S(1)}, f32[96,128]{0,1:T(8,128)S(1)}, u32[]{:S(2)}, u32[]{:S(2)}) collective-permute-start(f32[96,128]{0,1:T(8,128)S(1)} %get-tuple-element.132), channel_id=1, source_target_pairs={{0,1},{1,2},{2,3},{3,4},{4,5},{5,6},{6,7},{8,9},{9,10},{10,11},{11... | collective-permute-start | bytes 147464 | tf_op jit(solution)/shard_map/ppermute | solution.py:29
  (2 other events, 2.2 us)
Sparse Core Ops, SparseCore 0:
  148.3 34.7 reduce-scatter.2
  185.3 28.7 reduce-scatter.4
where the time goes:
time: 223 us; the launch traced here: 222 us
  waiting for transfers between devices  76.2 us (34%)
  starting transfers between devices  56 us (25%)
  other arithmetic  38.9 us (17%)
  local copies, waits for them, and re-layouts  20.2 us (9%)
  between operations  14.8 us (7%)
  blocking collectives  12.1 us (5%)
  matrix products  4.05 us (2%)
    scatter-add x5, other arithmetic, apply_hamiltonian(): summed.at[:, local_index.reshape(-1)]  30.9 us
    ppermute x10, starting transfers between devices, shifted(): return lax.ppermute(block, axis, route)  30.6 us
    reduce_scatter x1, waiting for transfers between devices, per_device(): lax.psum_scatter(projected.astype(jnp.bfloat16), 'space', scatter_dimensi...  29.7 us
    reduce_scatter x1, waiting for transfers between devices, per_device(): lax.psum_scatter(intersection.astype(jnp.bfloat16), 'space', scatter_dime...  28.2 us
    ppermute x5, starting transfers between devices, padded(): before = lax.ppermute(last, axis, up)  18.7 us
    gather x10, local copies, waits for them, and re-layouts, apply_hamiltonian(): picked = extended[:, local_index]  16.7 us
    ppermute x5, waiting for transfers between devices, padded(): after = lax.ppermute(leading, axis, down)  14 us
    all_gather x1, blocking collectives, per_device(): incoming = lax.all_gather(current, 'state', axis=0, tiled=True)  12.1 us
  transfers between devices with their start and end apart: 22, of which 11 were waited for; matrix products, arithmetic and copies ran while one was open for 2% of the time, Pallas kernels for 0%

commit v1 on v0

v1 whole, which is shorter than its diff:
```python
import functools

import jax
import jax.numpy as jnp
from jax import lax
from jax.experimental import pallas as pl
from jax.experimental.pallas import tpu as pltpu
from jax.sharding import PartitionSpec as P

DEGREE = 4

spectrum_center = 3.0
spectrum_half = 3.5

BF16 = jnp.bfloat16
F32 = jnp.float32


def call(body, outs, flops, n_in, smem_first=True, aliases=None, scratch=(), moved=4 << 20):
    specs = [pl.BlockSpec(memory_space=pltpu.VMEM)] * n_in
    if smem_first:
        specs = [pl.BlockSpec(memory_space=pltpu.SMEM)] + specs
    return pl.pallas_call(
        body,
        out_shape=outs,
        in_specs=specs,
        out_specs=jax.tree.map(lambda _: pl.BlockSpec(memory_space=pltpu.VMEM), outs),
        scratch_shapes=list(scratch),
        input_output_aliases=aliases or {},
        compiler_params=pltpu.CompilerParams(vmem_limit_bytes=24 << 20),
        cost_estimate=pl.CostEstimate(flops=flops, bytes_accessed=moved, transcendentals=0),
    )


def assemble_body(cells_ref, row_ref, col_ref, matrix_ref, diagonal_ref, wide_ref):
    cells, nodes, _ = cells_ref.shape
    extent = matrix_ref.shape[0]
    step = 256
    for c in range(cells):
        hot = lax.broadcasted_iota(jnp.int32, (extent, nodes), 0) == row_ref[c : c + 1, :]
        half = jnp.dot(hot.astype(BF16), cells_ref[c], preferred_element_type=F32)
        wide_ref[:, c * nodes : (c + 1) * nodes] = half.astype(BF16)
    spread = lax.broadcasted_iota(jnp.int32, (cells * nodes, extent), 1) == col_ref[...]
    spread = spread.astype(BF16)
    for start in range(0, extent, step):
        rows = jnp.dot(wide_ref[start : start + step, :], spread, preferred_element_type=F32)
        own = lax.broadcasted_iota(jnp.int32, rows.shape, 0) + start == lax.broadcasted_iota(
            jnp.int32, rows.shape, 1
        )
        piece = jnp.where(own, rows, 0.0)
        diagonal_ref[:, start : start + step] = jnp.sum(
            piece[:, start : start + step], axis=0, keepdims=True
        )
        matrix_ref[start : start + step, :] = jnp.where(own, 0.0, rows).astype(BF16)


def assemble(cell_matrices, local_index, extent):
    cells, nodes, _ = cell_matrices.shape
    outs = (
        jax.ShapeDtypeStruct((extent, extent), BF16),
        jax.ShapeDtypeStruct((1, extent), F32),
    )
    return call(
        assemble_body,
        outs,
        2 * extent * nodes * cells * (nodes + extent),
        3,
        smem_first=False,
        scratch=[pltpu.VMEM((extent, cells * nodes), BF16)],
    )(cell_matrices, local_index, local_index.reshape(-1, 1))


def pick(low_first, low, high):
    return jnp.where(low_first, low, high)


def apply_to(level_ref, matrix_ref, diagonal_ref):
    level = level_ref[...]
    sums = jnp.dot(level, matrix_ref[...], preferred_element_type=F32)
    return sums + diagonal_ref[...] * level.astype(F32)


def finish_zones(place, width, own_ref, got_a_ref, got_b_ref, shift_ref, mid_ref, old_ref, scale, level_ref):
    extent = level_ref.shape[1]
    odd, first, last = place[0] == 1, place[1] == 1, place[2] == 1
    got_a, got_b = got_a_ref[...].astype(F32), got_b_ref[...].astype(F32)
    got_low = jnp.where(first, 0.0, jnp.where(odd, got_a, got_b))
    got_high = jnp.where(last, 0.0, jnp.where(odd, got_b, got_a))
    for got, mine, at in ((got_low, 0, 0), (got_high, width, extent - width)):
        here = slice(at, at + width)
        total = own_ref[:, mine : mine + width] + got
        value = (total + shift_ref[:, here] * mid_ref[:, here].astype(F32)) * scale
        if old_ref is not None:
            value = value - old_ref[:, here].astype(F32)
        level_ref[:, here] = value.astype(BF16)


def advance(place, width, level_ref, old_ref, matrix_ref, diagonal_ref, shift_ref, scale, following_ref, own_ref, give_a_ref, give_b_ref):
    extent = level_ref.shape[1]
    sums = apply_to(level_ref, matrix_ref, diagonal_ref)
    inside = slice(width, extent - width)
    value = (sums[:, inside] + shift_ref[:, inside] * level_ref[:, inside].astype(F32)) * scale
    if old_ref is not None:
        value = value - old_ref[:, inside].astype(F32)
    following_ref[:, inside] = value.astype(BF16)
    low, high = sums[:, :width], sums[:, extent - width :]
    own_ref[:, :width] = low
    own_ref[:, width:] = high
    odd = place[0] == 1
    give_a_ref[...] = jnp.where(odd, low, high).astype(BF16)
    give_b_ref[...] = jnp.where(odd, high, low).astype(BF16)


def first_body(place, states_ref, halo_a_ref, halo_b_ref, potential_ref, matrix_ref, diagonal_ref,
               level_ref, shift_ref, following_ref, own_ref, give_a_ref, give_b_ref):
    count, owned = states_ref.shape
    extent = level_ref.shape[1]
    rim = (extent - owned) // 2
    odd, first, last = place[0] == 1, place[1] == 1, place[2] == 1
    got_a, got_b = halo_a_ref[...].astype(F32), halo_b_ref[...].astype(F32)
    got_low = jnp.where(first, 0.0, jnp.where(odd, got_a, got_b))
    got_high = jnp.where(last, 0.0, jnp.where(odd, got_b, got_a))
    level_ref[:, rim : rim + owned] = states_ref[...]
    level_ref[:, :rim] = got_low[:count].astype(BF16)
    level_ref[:, rim + owned :] = got_high[:count].astype(BF16)
    shift_ref[:, rim : rim + owned] = potential_ref[...] - spectrum_center
    for got, at in ((got_low, 0), (got_high, rim + owned)):
        parts = got[count : count + 8]
        value = parts[0:1] + parts[1:2] + parts[2:3]
        shift_ref[:, at : at + rim] = value - spectrum_center
    advance(place, 2 * rim, level_ref, None, matrix_ref, diagonal_ref, shift_ref, 1.0 / spectrum_half,
            following_ref, own_ref, give_a_ref, give_b_ref)


def middle_body(with_old, place, own_ref, got_a_ref, got_b_ref, open_ref, mid_ref, *rest):
    if with_old:
        old_ref, *rest = rest
    else:
        old_ref = None
    (shift_ref, matrix_ref, diagonal_ref,
     level_ref, following_ref, next_own_ref, give_a_ref, give_b_ref) = rest
    width = got_a_ref.shape[1]
    extent = mid_ref.shape[1]
    scale = (2.0 if with_old else 1.0) / spectrum_half
    inside = slice(width, extent - width)
    level_ref[:, inside] = open_ref[:, inside]
    finish_zones(place, width, own_ref, got_a_ref, got_b_ref, shift_ref, mid_ref, old_ref, scale, level_ref)
    advance(place, width, level_ref, mid_ref, matrix_ref, diagonal_ref, shift_ref, 2.0 / spectrum_half,
            following_ref, next_own_ref, give_a_ref, give_b_ref)


def last_body(place, own_ref, got_a_ref, got_b_ref, open_ref, mid_ref, old_ref, shift_ref, level_ref, filtered_ref):
    width = got_a_ref.shape[1]
    extent = mid_ref.shape[1]
    rim = width // 2
    inside = slice(width, extent - width)
    level_ref[:, inside] = open_ref[:, inside]
    finish_zones(place, width, own_ref, got_a_ref, got_b_ref, shift_ref, mid_ref, old_ref,
                 2.0 / spectrum_half, level_ref)
    filtered_ref[...] = level_ref[:, rim : extent - rim]


def energy_body(place, level_ref, matrix_ref, diagonal_ref, shift_ref, energy_ref, give_a_ref, give_b_ref):
    extent = level_ref.shape[1]
    owned = energy_ref.shape[1]
    rim = (extent - owned) // 2
    sums = apply_to(level_ref, matrix_ref, diagonal_ref)
    here = slice(rim, rim + owned)
    energy_ref[...] = sums[:, here] + (shift_ref[:, here] + spectrum_center) * level_ref[:, here].astype(F32)
    low, high = sums[:, :rim], sums[:, rim + owned :]
    odd = place[0] == 1
    give_a_ref[...] = jnp.where(odd, low, high).astype(BF16)
    give_b_ref[...] = jnp.where(odd, high, low).astype(BF16)


def project_body(total_nodes, groups, place, energy_ref, got_a_ref, got_b_ref, *refs):
    blocks, out_ref, pair_ref = refs[:groups], refs[groups], refs[groups + 1]
    count, owned = energy_ref.shape
    rim = got_a_ref.shape[1]
    odd, first, last = place[0] == 1, place[1] == 1, place[2] == 1
    got_a, got_b = got_a_ref[...].astype(F32), got_b_ref[...].astype(F32)
    got_low = jnp.where(first, 0.0, jnp.where(odd, got_a, got_b))
    got_high = jnp.where(last, 0.0, jnp.where(odd, got_b, got_a))
    pair_ref[:count, :] = blocks[0][...]
    pair_ref[count:, :rim] = (energy_ref[:, :rim] + got_low).astype(BF16)
    pair_ref[count:, rim : owned - rim] = energy_ref[:, rim : owned - rim].astype(BF16)
    pair_ref[count:, owned - rim :] = (energy_ref[:, owned - rim :] + got_high).astype(BF16)
    group = place[3]
    pair = pair_ref[...]
    for distance in range(groups):
        part = lax.dot_general(
            blocks[distance][...], pair, (((1,), (1,)), ((), ())), preferred_element_type=F32
        )
        at = pl.multiple_of((group ^ distance) * count, count)
        out_ref[pl.ds(at, count), :] = (part * (1.0 / total_nodes)).astype(BF16)


def halve_body(place, mine_ref, got_ref, sum_ref):
    core = place[0]
    for j in range(sum_ref.shape[0]):
        mine = jnp.where(core == 1, mine_ref[j, 1].astype(F32), mine_ref[j, 0].astype(F32))
        sum_ref[j] = (mine + got_ref[j].astype(F32)).astype(BF16)


def final_body(count, *refs):
    parts, (first_ref, second_ref) = refs[:-2], refs[-2:]
    total = parts[0][...].astype(F32)
    for part in parts[1:]:
        total = total + part[...].astype(F32)
    first_ref[...] = total[:, :count].T
    second_ref[...] = total[:, count:].T


def swap(block, n_state, n_space, lead):
    route = []
    for s in range(n_state):
        for i in range(n_space):
            j = i + 1 if (i - lead) % 2 == 0 else i - 1
            if 0 <= j < n_space:
                route.append((s * n_space + i, s * n_space + j))
            elif (s ^ 1) < n_state:
                route.append((s * n_space + i, (s ^ 1) * n_space + i))
    return lax.ppermute(block, ("state", "space"), route)


def exchange(pair, n_state, n_space):
    give_a, give_b = pair
    got_b = swap(give_b, n_state, n_space, 1)
    got_a = swap(give_a, n_state, n_space, 0)
    return got_a, got_b


def across(block, axis, distance):
    return lax.ppermute(block, axis, [(i, i ^ distance) for i in range(lax.axis_size(axis))])


def three_parts(row):
    high = lax.reduce_precision(row, 8, 7)
    mid = lax.reduce_precision(row - high, 8, 7)
    low = (row - high) - mid
    return jnp.concatenate([high, mid, low], axis=0).astype(BF16)


def per_device(states_in, cell_matrices, connectivity, potential):
    count, owned = states_in.shape
    rim = cell_matrices.shape[1] // 4
    extent = owned + 2 * rim
    n_state, n_space = lax.axis_size("state"), lax.axis_size("space")
    me = lax.axis_index("space")
    group = lax.axis_index("state")
    odd = me % 2
    place = jnp.stack(
        [odd, (me == 0).astype(jnp.int32), (me == n_space - 1).astype(jnp.int32), group]
    ).astype(jnp.int32)
    local_index = connectivity - (me * owned - rim)

    row = potential.reshape(1, owned)
    parts = three_parts(row)
    parts = jnp.concatenate([parts, jnp.zeros((13, owned), BF16)], axis=0)
    low = jnp.concatenate([states_in[:, :rim], parts[:, :rim]], axis=0)
    high = jnp.concatenate([states_in[:, owned - rim :], parts[:, owned - rim :]], axis=0)
    halo = exchange(
        (jnp.where(odd == 1, low, high), jnp.where(odd == 1, high, low)), n_state, n_space
    )
    matrix, diagonal = assemble(cell_matrices, local_index, extent)

    shape = jax.ShapeDtypeStruct
    wide, line = shape((count, extent), BF16), shape((1, extent), F32)
    own, give = shape((count, 4 * rim), F32), shape((count, 2 * rim), BF16)
    flops = 2 * count * extent * extent
    start, shift, opened, sums, *gave = call(
        first_body, (wide, line, wide, own, give, give), flops, 6
    )(place, states_in, *halo, row, matrix, diagonal)
    levels = [start]
    for k in range(1, DEGREE):
        got = exchange(gave, n_state, n_space)
        older = levels[-2:-1]
        level, opened, sums, *gave = call(
            functools.partial(middle_body, bool(older)),
            (wide, wide, own, give, give), flops, 8 + len(older),
        )(place, sums, *got, opened, levels[-1], *older, shift, matrix, diagonal)
        levels.append(level)
    got = exchange(gave, n_state, n_space)
    level, filtered = call(last_body, (wide, shape((count, owned), BF16)), 0, 7)(
        place, sums, *got, opened, levels[-1], levels[-2], shift
    )
    rim_give = shape((count, rim), BF16)
    energy, *gave = call(
        energy_body, (shape((count, owned), F32), rim_give, rim_give), flops, 4
    )(place, level, matrix, diagonal, shift)
    blocks = [filtered] + [across(filtered, "state", d) for d in range(1, n_state)]
    got = exchange(gave, n_state, n_space)
    total_states = count * n_state
    partial = call(
        functools.partial(project_body, owned * n_space, n_state),
        shape((total_states, 2 * count), BF16), 2 * total_states * 2 * count * owned, 3 + n_state,
        scratch=[pltpu.VMEM((2 * count, owned), BF16)],
    )(place, energy, *got, *blocks)

    columns = total_states // n_space
    partial = partial.reshape(n_space // 2, 2, columns, 2 * count)
    give = jnp.where(odd == 1, partial[:, 0], partial[:, 1])
    got = swap(give, n_state, n_space, 0)
    halved = call(halve_body, shape(give.shape, BF16), 0, 2)(place, partial, got)
    chip = me // 2
    pieces = [
        lax.dynamic_index_in_dim(halved, chip ^ d, 0, keepdims=False) for d in range(n_space // 2)
    ]
    pieces = [pieces[0]] + [across(p, "space", 2 * d) for d, p in enumerate(pieces) if d]
    square = shape((count, columns), F32)
    intersection, projected = call(
        functools.partial(final_body, count), (square, square), 0, len(pieces), smem_first=False
    )(*pieces)
    return filtered, intersection, projected


def solution(mesh):
    return jax.shard_map(
        per_device,
        mesh=mesh,
        in_specs=(P("state", "space"), P("space", None, None), P("space", None), P("space")),
        out_specs=(P("state", "space"), P("state", "space"), P("state", "space")),
        check_vma=False,
    )
```

time: 223 us -> 60.9 us (0.27)
  waiting for transfers between devices: 76.2 us -> 20.7 us
  starting transfers between devices: 56 us -> 18.7 us
  other arithmetic: 38.9 us -> 2.21 us
  local copies, waits for them, and re-layouts: 20.2 us -> 3.64 us
  Pallas kernels: 0 us -> 14.4 us
  between operations: 14.8 us -> 0.88 us
  blocking collectives: 12.1 us -> 0 us
  matrix products: 4.05 us -> 0 us
    reduce_scatter x2 -> x0, waiting for transfers between devices: 57.8 us -> none  [the longest x1 29.7 us: per_device(): lax.psum_scatter(projected.astype(jnp.bfloat16), 'space', scatter_dimensi...]
    ppermute x20 -> x19, starting transfers between devices: 56 us -> 18.7 us  [the longest x13 10.8 us: swap(): return lax.ppermute(block, ('state', 'space'), route)]
    scatter-add x15 -> x0, other arithmetic: 34.3 us -> none  [the longest x5 30.9 us: apply_hamiltonian(): summed.at[:, local_index.reshape(-1)]]
    gather x10 -> x0, local copies, waits for them, and re-layouts: 16.7 us -> none  [apply_hamiltonian(): picked = extended[:, local_index]]
    pallas_call x0 -> x10, Pallas kernels: none -> 14.4 us  [the longest x1 5.13 us: assemble(): call(assemble_body, outs, 2 * extent * nodes * cells * (nodes + extent),...]
    all_gather x1 -> x0, blocking collectives: 12.1 us -> none  [per_device(): incoming = lax.all_gather(current, 'state', axis=0, tiled=True)]
    dot_general x7 -> x0, matrix products: 4.05 us -> none  [the longest x1 1.54 us: per_device(): lax.dot_general(energy, incoming.astype(jnp.float32), contract, precision...]
    convert_element_type x6 -> x0, other arithmetic: 3.64 us -> none  [the longest x2 2.63 us: per_device(): intersection, projected = (lax.psum_scatter(intersection.astype(jnp.bfloa...]
  transfers between devices with their start and end apart: 22 -> 19, of which waited for: 11 -> 8; matrix products, arithmetic and copies ran while one was open for 2% -> 3% of each run, Pallas kernels for 0% -> 10%
where the time goes in v1:
time: 60.9 us; the launch traced here: 60.6 us
  waiting for transfers between devices  20.7 us (34%)
  starting transfers between devices  18.7 us (31%)
  Pallas kernels  14.4 us (24%)
  local copies, waits for them, and re-layouts  3.64 us (6%)
  other arithmetic  2.21 us (4%)
  between operations  0.88 us (1%)
    ppermute x13, waiting for transfers between devices, swap(): return lax.ppermute(block, ('state', 'space'), route)  18.9 us
    ppermute x13, starting transfers between devices, swap(): return lax.ppermute(block, ('state', 'space'), route)  10.8 us
    ppermute x6, starting transfers between devices, across(): lax.ppermute(block, axis, [(i, i ^ distance) for i in range(lax.axis_size...  7.94 us
    pallas_call x1, Pallas kernels, assemble(): call(assemble_body, outs, 2 * extent * nodes * cells * (nodes + extent),...  5.13 us
    pallas_call x3, Pallas kernels, per_device(): call(functools.partial(middle_body, bool(older)), (wide, wide, own, give,...  3.62 us
    unnamed x12, local copies, waits for them, and re-layouts  2.84 us
    ppermute x6, waiting for transfers between devices, across(): lax.ppermute(block, axis, [(i, i ^ distance) for i in range(lax.axis_size...  1.81 us
    pallas_call x1, Pallas kernels, per_device(): call(last_body, (wide, shape((count, owned), BF16)), 0, 7)  1.31 us
  transfers between devices with their start and end apart: 19, of which 8 were waited for; matrix products, arithmetic and copies ran while one was open for 3% of the time, Pallas kernels for 10%

profile of v1, /device:TPU:0, one launch (start us, length us, event | category | flops | bytes accessed | tf_op | source)
XLA Modules:
  0.0 60.6 jit_solution(7448303204238160012)
XLA Ops:
  2.2 3.0 %collective-permute-start.1 = (bf16[112,128]{1,0:T(8,128)(2,1)S(1)}, bf16[112,128]{1,0:T(8,128)(2,1)S(1)}, u32[]{:S(2)}, u32[]{:S(2)}) collective-permute-start(bf16[112,128]{1,0:T(8,128)(2,1)S(1)} %get-tuple-element.75), channel_id=1, source_target_pairs={{0,8},{1,2},{2,1},{3,4},{4,3},{5,6},{6,5},{7,15},{8,0},{9,10},{10,... | collective-permute-start | bytes 86024 | tf_op jit(solution)/shard_map/ppermute | solution.py:223
  7.1 1.2 %copy-done.3 = bf16[2,512,512]{2,1,0:T(8,128)(2,1)S(1)} copy-done((bf16[2,512,512]{2,1,0:T(8,128)(2,1)S(1)}, bf16[2,512,512]{2,1,0:T(8,128)(2,1)}, u32[]{:S(2)}) %copy-start.3) | copy-done | bytes 1048600
  8.3 5.1 %shard_map.67 = (bf16[1280,1280]{1,0:T(8,128)(2,1)S(1)}, f32[1,1280]{1,0:T(1,128)S(1)}) custom-call(bf16[2,512,512]{2,1,0:T(8,128)(2,1)S(1)} %copy-done.3, s32[2,512]{1,0:T(2,128)S(1)} %broadcast_subtract_fusion.row_ref, s32[1024,1]{1,0:T(8,128)S(1)} %bitcast.33), custom_call_target="tpu_custom_call" | custom-call | flops 4697620480 | bytes 4194304 | tf_op jit(solution)/shard_map/pallas_call | solution.py:63
  13.5 1.2 %shard_map.68 = (bf16[96,1280]{1,0:T(8,128)(2,1)S(1)}, f32[1,1280]{1,0:T(1,128)S(1)}, bf16[96,1280]{1,0:T(8,128)(2,1)S(1)}, f32[96,512]{1,0:T(8,128)S(1)}, bf16[...) custom-call(s32[4]{0:T(128)S(1)} %pad_add_fusion.place, bf16[96,1024]{1,0:T(8,128)(2,1)S(1)} %copy-done, ...), custom_call_target="tpu_custom_call" | custom-call | flops 314572800 | bytes 4194304 | tf_op jit(solution)/shard_map/pallas_call | solution.py:271
  15.1 1.3 %collective-permute-start.3 = (bf16[96,256]{1,0:T(8,128)(2,1)S(1)}, bf16[96,256]{1,0:T(8,128)(2,1)S(1)}, u32[]{:S(2)}, u32[]{:S(2)}) collective-permute-start(bf16[96,256]{1,0:T(8,128)(2,1)S(1)} %get-tuple-element.37), channel_id=1, source_target_pairs={{0,8},{1,2},{2,1},{3,4},{4,3},{5,6},{6,5},{7,15},{8,0},{9,10},{10,... | collective-permute-start | bytes 147464 | tf_op jit(solution)/shard_map/ppermute | solution.py:223
  16.4 2.8 %collective-permute-done.3.got_b_ref = bf16[96,256]{1,0:T(8,128)(2,1)S(1)} collective-permute-done((bf16[96,256]{1,0:T(8,128)(2,1)S(1)}, bf16[96,256]{1,0:T(8,128)(2,1)S(1)}, u32[]{:S(2)}, u32[]{:S(2)}) %collective-permute-start.3) | collective-permute-done | bytes 49184 | tf_op jit(solution)/shard_map/ppermute | solution.py:223
  19.2 1.2 %shard_map.69 = (bf16[96,1280]{1,0:T(8,128)(2,1)S(1)}, bf16[96,1280]{1,0:T(8,128)(2,1)S(1)}, f32[96,512]{1,0:T(8,128)S(1)}, bf16[96,256]{1,0:T(8,128)(2,1)S(1)}, bf16[96,256]{1,0:T(8,128)(2,1)S(1)}) custom-call(s32[4]{0:T(128)S(1)} %pad_add_fusion.place, f32[96,512]{1,0:T(8,128)S(1)} %get-tuple-element.35.own_ref, ...), custom_call_target="tpu_custom_call" | custom-call | flops 314572800 | bytes 4194304 | tf_op jit(solution)/shard_map/pallas_call | solution.py:278
  20.5 1.4 %collective-permute-start.5 = (bf16[96,256]{1,0:T(8,128)(2,1)S(1)}, bf16[96,256]{1,0:T(8,128)(2,1)S(1)}, u32[]{:S(2)}, u32[]{:S(2)}) collective-permute-start(bf16[96,256]{1,0:T(8,128)(2,1)S(1)} %get-tuple-element.43), channel_id=1, source_target_pairs={{0,8},{1,2},{2,1},{3,4},{4,3},{5,6},{6,5},{7,15},{8,0},{9,10},{10,... | collective-permute-start | bytes 147464 | tf_op jit(solution)/shard_map/ppermute | solution.py:223
  21.9 2.8 %collective-permute-done.5.got_b_ref = bf16[96,256]{1,0:T(8,128)(2,1)S(1)} collective-permute-done((bf16[96,256]{1,0:T(8,128)(2,1)S(1)}, bf16[96,256]{1,0:T(8,128)(2,1)S(1)}, u32[]{:S(2)}, u32[]{:S(2)}) %collective-permute-start.5) | collective-permute-done | bytes 49184 | tf_op jit(solution)/shard_map/ppermute | solution.py:223
  24.7 1.2 %shard_map.70 = (bf16[96,1280]{1,0:T(8,128)(2,1)S(1)}, bf16[96,1280]{1,0:T(8,128)(2,1)S(1)}, f32[96,512]{1,0:T(8,128)S(1)}, bf16[96,256]{1,0:T(8,128)(2,1)S(1)}, bf16[96,256]{1,0:T(8,128)(2,1)S(1)}) custom-call(s32[4]{0:T(128)S(1)} %pad_add_fusion.place, f32[96,512]{1,0:T(8,128)S(1)} %get-tuple-element.41.own_ref, ...), custom_call_target="tpu_custom_call" | custom-call | flops 314572800 | bytes 4194304 | tf_op jit(solution)/shard_map/pallas_call | solution.py:278
  26.1 1.3 %collective-permute-start.7 = (bf16[96,256]{1,0:T(8,128)(2,1)S(1)}, bf16[96,256]{1,0:T(8,128)(2,1)S(1)}, u32[]{:S(2)}, u32[]{:S(2)}) collective-permute-start(bf16[96,256]{1,0:T(8,128)(2,1)S(1)} %get-tuple-element.48), channel_id=1, source_target_pairs={{0,8},{1,2},{2,1},{3,4},{4,3},{5,6},{6,5},{7,15},{8,0},{9,10},{10,... | collective-permute-start | bytes 147464 | tf_op jit(solution)/shard_map/ppermute | solution.py:223
  27.4 2.8 %collective-permute-done.7.got_b_ref = bf16[96,256]{1,0:T(8,128)(2,1)S(1)} collective-permute-done((bf16[96,256]{1,0:T(8,128)(2,1)S(1)}, bf16[96,256]{1,0:T(8,128)(2,1)S(1)}, u32[]{:S(2)}, u32[]{:S(2)}) %collective-permute-start.7) | collective-permute-done | bytes 49184 | tf_op jit(solution)/shard_map/ppermute | solution.py:223
  30.2 1.2 %shard_map.71 = (bf16[96,1280]{1,0:T(8,128)(2,1)S(1)}, bf16[96,1280]{1,0:T(8,128)(2,1)S(1)}, f32[96,512]{1,0:T(8,128)S(1)}, bf16[96,256]{1,0:T(8,128)(2,1)S(1)}, bf16[96,256]{1,0:T(8,128)(2,1)S(1)}) custom-call(s32[4]{0:T(128)S(1)} %pad_add_fusion.place, f32[96,512]{1,0:T(8,128)S(1)} %get-tuple-element.46.own_ref, ...), custom_call_target="tpu_custom_call" | custom-call | flops 314572800 | bytes 4194304 | tf_op jit(solution)/shard_map/pallas_call | solution.py:278
  31.6 1.3 %collective-permute-start.9 = (bf16[96,256]{1,0:T(8,128)(2,1)S(1)}, bf16[96,256]{1,0:T(8,128)(2,1)S(1)}, u32[]{:S(2)}, u32[]{:S(2)}) collective-permute-start(bf16[96,256]{1,0:T(8,128)(2,1)S(1)} %get-tuple-element.53), channel_id=1, source_target_pairs={{0,8},{1,2},{2,1},{3,4},{4,3},{5,6},{6,5},{7,15},{8,0},{9,10},{10,... | collective-permute-start | bytes 147464 | tf_op jit(solution)/shard_map/ppermute | solution.py:223
  32.9 2.8 %collective-permute-done.9.got_b_ref = bf16[96,256]{1,0:T(8,128)(2,1)S(1)} collective-permute-done((bf16[96,256]{1,0:T(8,128)(2,1)S(1)}, bf16[96,256]{1,0:T(8,128)(2,1)S(1)}, u32[]{:S(2)}, u32[]{:S(2)}) %collective-permute-start.9) | collective-permute-done | bytes 49184 | tf_op jit(solution)/shard_map/ppermute | solution.py:223
  35.7 1.3 %shard_map.72 = (bf16[96,1280]{1,0:T(8,128)(2,1)S(1)}, bf16[96,1024]{1,0:T(8,128)(2,1)}) custom-call(s32[4]{0:T(128)S(1)} %pad_add_fusion.place, f32[96,512]{1,0:T(8,128)S(1)} %get-tuple-element.51.own_ref, bf16[96,256]{1,0:T(8,128)(2,1)S(1)} %collective-permute-done.8.got_a_ref, bf16[96,256]{1,0:T(8,128)(2,1)S(1)} %collective-permute-done.9.got_b_ref, ...), custom_call_target="tpu_custom_call" | custom-call | bytes 4194304 | tf_op jit(solution)/shard_map/pallas_call | solution.py:284
  37.0 2.3 %collective-permute-start.14 = (bf16[96,1024]{1,0:T(8,128)(2,1)}, bf16[96,1024]{1,0:T(8,128)(2,1)S(1)}, u32[]{:S(2)}, u32[]{:S(2)}) collective-permute-start(bf16[96,1024]{1,0:T(8,128)(2,1)} %get-tuple-element.66.refs_0_), channel_id=1, source_target_pairs={{0,24},{8,16},{16,8},{24,0},{1,25},{9,17},{17,9},{25,1},{2,26},{10... | collective-permute-start | bytes 589832 | tf_op jit(solution)/shard_map/ppermute | solution.py:234
  40.5 1.2 %shard_map.73 = (f32[96,1024]{1,0:T(8,128)S(1)}, bf16[96,128]{1,0:T(8,128)(2,1)S(1)}, bf16[96,128]{1,0:T(8,128)(2,1)S(1)}) custom-call(s32[4]{0:T(128)S(1)} %pad_add_fusion.place, bf16[96,1280]{1,0:T(8,128)(2,1)S(1)} %get-tuple-element.57.level_ref, bf16[1280,1280]{1,0:T(8,128)(2,1)S(1)} %get-tuple-element.33.matrix_ref.rest_1_.rest_2_, ...), custom_call_target="tpu_custom_call" | custom-call | flops 314572800 | bytes 4194304 | tf_op jit(solution)/shard_map/pallas_call | solution.py:288
  41.8 1.4 %collective-permute-start.11 = (bf16[96,128]{1,0:T(8,128)(2,1)S(1)}, bf16[96,128]{1,0:T(8,128)(2,1)S(1)}, u32[]{:S(2)}, u32[]{:S(2)}) collective-permute-start(bf16[96,128]{1,0:T(8,128)(2,1)S(1)} %get-tuple-element.60), channel_id=1, source_target_pairs={{0,8},{1,2},{2,1},{3,4},{4,3},{5,6},{6,5},{7,15},{8,0},{9,10},{10,... | collective-permute-start | bytes 73736 | tf_op jit(solution)/shard_map/ppermute | solution.py:223
  43.1 6.5 %collective-permute-done.11.got_b_ref = bf16[96,128]{1,0:T(8,128)(2,1)S(1)} collective-permute-done((bf16[96,128]{1,0:T(8,128)(2,1)S(1)}, bf16[96,128]{1,0:T(8,128)(2,1)S(1)}, u32[]{:S(2)}, u32[]{:S(2)}) %collective-permute-start.11) | collective-permute-done | bytes 24608 | tf_op jit(solution)/shard_map/ppermute | solution.py:223
  49.6 1.2 %shard_map.74 = bf16[384,192]{1,0:T(8,128)(2,1)S(1)} custom-call(s32[4]{0:T(128)S(1)} %pad_add_fusion.place, f32[96,1024]{1,0:T(8,128)S(1)} %get-tuple-element.58.energy_ref, bf16[96,128]{1,0:T(8,128)(2,1)S(1)} %collective-permute-done.10.got_a_ref, bf16[96,128]{1,0:T(8,128)(2,1)S(1)} %collective-permute-done.11.got_b_ref, bf16[96,1024]{1,0:T(8,128)(2,1)S(1)} %copy-done.1, ...), custom_call_target="tpu_custom_call" | custom-call | flops 150994944 | bytes 4194304 | tf_op jit(solution)/shard_map/pallas_call | solution.py:294
  51.0 1.3 %collective-permute-done.15.got_ref = bf16[4,48,192]{2,1,0:T(8,128)(2,1)S(1)} collective-permute-done((bf16[4,48,192]{2,1,0:T(8,128)(2,1)S(1)}, bf16[4,48,192]{2,1,0:T(8,128)(2,1)S(1)}, u32[]{:S(2)}, u32[]{:S(2)}) %collective-permute-start.15) | collective-permute-done | bytes 73760 | tf_op jit(solution)/shard_map/ppermute | solution.py:223
  53.8 3.5 %collective-permute-start.16 = (bf16[48,192]{1,0:T(8,128)(2,1)S(1)}, bf16[48,192]{1,0:T(8,128)(2,1)S(1)}, u32[]{:S(2)}, u32[]{:S(2)}) collective-permute-start(bf16[48,192]{1,0:T(8,128)(2,1)S(1)} %get-tuple-element.73), channel_id=1, source_target_pairs={{0,2},{1,3},{2,0},{3,1},{4,6},{5,7},{6,4},{7,5},{8,10},{9,11},{10,... | collective-permute-start | bytes 55304 | tf_op jit(solution)/shard_map/ppermute | solution.py:234
  57.3 1.2 %collective-permute-done.18.refs_3_ = bf16[48,192]{1,0:T(8,128)(2,1)S(1)} collective-permute-done((bf16[48,192]{1,0:T(8,128)(2,1)S(1)}, bf16[48,192]{1,0:T(8,128)(2,1)S(1)}, u32[]{:S(2)}, u32[]{:S(2)}) %collective-permute-start.18) | collective-permute-done | bytes 18464 | tf_op jit(solution)/shard_map/ppermute | solution.py:234
  (49 shorter events, 9.3 us)
Async XLA Ops:
  2.2 11.3 %collective-permute-start.1 = (bf16[112,128]{1,0:T(8,128)(2,1)S(1)}, bf16[112,128]{1,0:T(8,128)(2,1)S(1)}, u32[]{:S(2)}, u32[]{:S(2)}) collective-permute-start(bf16[112,128]{1,0:T(8,128)(2,1)S(1)} %get-tuple-element.75), channel_id=1, source_target_pairs={{0,8},{1,2},{2,1},{3,4},{4,3},{5,6},{6,5},{7,15},{8,0},{9,10},{10,... | collective-permute-start | bytes 86024 | tf_op jit(solution)/shard_map/ppermute | solution.py:223
  5.2 8.3 %collective-permute-start = (bf16[112,128]{1,0:T(8,128)(2,1)S(1)}, bf16[112,128]{1,0:T(8,128)(2,1)S(1)}, u32[]{:S(2)}, u32[]{:S(2)}) collective-permute-start(bf16[112,128]{1,0:T(8,128)(2,1)S(1)} %get-tuple-element.76), channel_id=1, source_target_pairs={{0,1},{1,0},{2,3},{3,2},{4,5},{5,4},{6,7},{7,6},{8,9},{9,8},{10,11... | collective-permute-start | bytes 86024 | tf_op jit(solution)/shard_map/ppermute | solution.py:223
  7.0 1.2 %copy-start.3 = (bf16[2,512,512]{2,1,0:T(8,128)(2,1)S(1)}, bf16[2,512,512]{2,1,0:T(8,128)(2,1)}, u32[]{:S(2)}) copy-start(bf16[2,512,512]{2,1,0:T(8,128)(2,1)} %cells_ref.1) | copy-start | bytes 3145732
  8.3 5.2 %copy-start = (bf16[96,1024]{1,0:T(8,128)(2,1)S(1)}, bf16[96,1024]{1,0:T(8,128)(2,1)}, u32[]{:S(2)}) copy-start(bf16[96,1024]{1,0:T(8,128)(2,1)} %states_ref.1) | copy-start | bytes 589828
  8.3 5.2 %copy-start.2 = (f32[1024]{0:T(1024)S(1)}, f32[1024]{0:T(1024)}, u32[]{:S(2)}) copy-start(f32[1024]{0:T(1024)} %param.7) | copy-start | bytes 12292
  14.8 1.6 %collective-permute-start.2 = (bf16[96,256]{1,0:T(8,128)(2,1)S(1)}, bf16[96,256]{1,0:T(8,128)(2,1)S(1)}, u32[]{:S(2)}, u32[]{:S(2)}) collective-permute-start(bf16[96,256]{1,0:T(8,128)(2,1)S(1)} %get-tuple-element.36), channel_id=1, source_target_pairs={{0,1},{1,0},{2,3},{3,2},{4,5},{5,4},{6,7},{7,6},{8,9},{9,8},{10,11... | collective-permute-start | bytes 147464 | tf_op jit(solution)/shard_map/ppermute | solution.py:223
  15.1 4.1 %collective-permute-start.3 = (bf16[96,256]{1,0:T(8,128)(2,1)S(1)}, bf16[96,256]{1,0:T(8,128)(2,1)S(1)}, u32[]{:S(2)}, u32[]{:S(2)}) collective-permute-start(bf16[96,256]{1,0:T(8,128)(2,1)S(1)} %get-tuple-element.37), channel_id=1, source_target_pairs={{0,8},{1,2},{2,1},{3,4},{4,3},{5,6},{6,5},{7,15},{8,0},{9,10},{10,... | collective-permute-start | bytes 147464 | tf_op jit(solution)/shard_map/ppermute | solution.py:223
  20.4 1.4 %collective-permute-start.4 = (bf16[96,256]{1,0:T(8,128)(2,1)S(1)}, bf16[96,256]{1,0:T(8,128)(2,1)S(1)}, u32[]{:S(2)}, u32[]{:S(2)}) collective-permute-start(bf16[96,256]{1,0:T(8,128)(2,1)S(1)} %get-tuple-element.42), channel_id=1, source_target_pairs={{0,1},{1,0},{2,3},{3,2},{4,5},{5,4},{6,7},{7,6},{8,9},{9,8},{10,11... | collective-permute-start | bytes 147464 | tf_op jit(solution)/shard_map/ppermute | solution.py:223
  20.5 4.2 %collective-permute-start.5 = (bf16[96,256]{1,0:T(8,128)(2,1)S(1)}, bf16[96,256]{1,0:T(8,128)(2,1)S(1)}, u32[]{:S(2)}, u32[]{:S(2)}) collective-permute-start(bf16[96,256]{1,0:T(8,128)(2,1)S(1)} %get-tuple-element.43), channel_id=1, source_target_pairs={{0,8},{1,2},{2,1},{3,4},{4,3},{5,6},{6,5},{7,15},{8,0},{9,10},{10,... | collective-permute-start | bytes 147464 | tf_op jit(solution)/shard_map/ppermute | solution.py:223
  25.9 1.5 %collective-permute-start.6 = (bf16[96,256]{1,0:T(8,128)(2,1)S(1)}, bf16[96,256]{1,0:T(8,128)(2,1)S(1)}, u32[]{:S(2)}, u32[]{:S(2)}) collective-permute-start(bf16[96,256]{1,0:T(8,128)(2,1)S(1)} %get-tuple-element.47), channel_id=1, source_target_pairs={{0,1},{1,0},{2,3},{3,2},{4,5},{5,4},{6,7},{7,6},{8,9},{9,8},{10,11... | collective-permute-start | bytes 147464 | tf_op jit(solution)/shard_map/ppermute | solution.py:223
  26.1 4.1 %collective-permute-start.7 = (bf16[96,256]{1,0:T(8,128)(2,1)S(1)}, bf16[96,256]{1,0:T(8,128)(2,1)S(1)}, u32[]{:S(2)}, u32[]{:S(2)}) collective-permute-start(bf16[96,256]{1,0:T(8,128)(2,1)S(1)} %get-tuple-element.48), channel_id=1, source_target_pairs={{0,8},{1,2},{2,1},{3,4},{4,3},{5,6},{6,5},{7,15},{8,0},{9,10},{10,... | collective-permute-start | bytes 147464 | tf_op jit(solution)/shard_map/ppermute | solution.py:223
  31.4 1.5 %collective-permute-start.8 = (bf16[96,256]{1,0:T(8,128)(2,1)S(1)}, bf16[96,256]{1,0:T(8,128)(2,1)S(1)}, u32[]{:S(2)}, u32[]{:S(2)}) collective-permute-start(bf16[96,256]{1,0:T(8,128)(2,1)S(1)} %get-tuple-element.52), channel_id=1, source_target_pairs={{0,1},{1,0},{2,3},{3,2},{4,5},{5,4},{6,7},{7,6},{8,9},{9,8},{10,11... | collective-permute-start | bytes 147464 | tf_op jit(solution)/shard_map/ppermute | solution.py:223
  31.6 4.1 %collective-permute-start.9 = (bf16[96,256]{1,0:T(8,128)(2,1)S(1)}, bf16[96,256]{1,0:T(8,128)(2,1)S(1)}, u32[]{:S(2)}, u32[]{:S(2)}) collective-permute-start(bf16[96,256]{1,0:T(8,128)(2,1)S(1)} %get-tuple-element.53), channel_id=1, source_target_pairs={{0,8},{1,2},{2,1},{3,4},{4,3},{5,6},{6,5},{7,15},{8,0},{9,10},{10,... | collective-permute-start | bytes 147464 | tf_op jit(solution)/shard_map/ppermute | solution.py:223
  37.0 12.6 %copy-start.1 = (bf16[96,1024]{1,0:T(8,128)(2,1)S(1)}, bf16[96,1024]{1,0:T(8,128)(2,1)}, u32[]{:S(2)}) copy-start(bf16[96,1024]{1,0:T(8,128)(2,1)} %get-tuple-element.66.refs_0_) | copy-start | bytes 589828
  37.0 12.6 %collective-permute-start.14 = (bf16[96,1024]{1,0:T(8,128)(2,1)}, bf16[96,1024]{1,0:T(8,128)(2,1)S(1)}, u32[]{:S(2)}, u32[]{:S(2)}) collective-permute-start(bf16[96,1024]{1,0:T(8,128)(2,1)} %get-tuple-element.66.refs_0_), channel_id=1, source_target_pairs={{0,24},{8,16},{16,8},{24,0},{1,25},{9,17},{17,9},{25,1},{2,26},{10... | collective-permute-start | bytes 589832 | tf_op jit(solution)/shard_map/ppermute | solution.py:234
  39.2 10.4 %collective-permute-start.13 = (bf16[96,1024]{1,0:T(8,128)(2,1)}, bf16[96,1024]{1,0:T(8,128)(2,1)S(1)}, u32[]{:S(2)}, u32[]{:S(2)}) collective-permute-start(bf16[96,1024]{1,0:T(8,128)(2,1)} %get-tuple-element.66.refs_0_), channel_id=1, source_target_pairs={{0,16},{8,24},{16,0},{24,8},{1,17},{9,25},{17,1},{25,9},{2,18},{10... | collective-permute-start | bytes 589832 | tf_op jit(solution)/shard_map/ppermute | solution.py:234
  39.7 9.9 %collective-permute-start.12 = (bf16[96,1024]{1,0:T(8,128)(2,1)}, bf16[96,1024]{1,0:T(8,128)(2,1)S(1)}, u32[]{:S(2)}, u32[]{:S(2)}) collective-permute-start(bf16[96,1024]{1,0:T(8,128)(2,1)} %get-tuple-element.66.refs_0_), channel_id=1, source_target_pairs={{0,8},{8,0},{16,24},{24,16},{1,9},{9,1},{17,25},{25,17},{2,10},{10... | collective-permute-start | bytes 589832 | tf_op jit(solution)/shard_map/ppermute | solution.py:234
  41.7 1.4 %collective-permute-start.10 = (bf16[96,128]{1,0:T(8,128)(2,1)S(1)}, bf16[96,128]{1,0:T(8,128)(2,1)S(1)}, u32[]{:S(2)}, u32[]{:S(2)}) collective-permute-start(bf16[96,128]{1,0:T(8,128)(2,1)S(1)} %get-tuple-element.59), channel_id=1, source_target_pairs={{0,1},{1,0},{2,3},{3,2},{4,5},{5,4},{6,7},{7,6},{8,9},{9,8},{10,11... | collective-permute-start | bytes 73736 | tf_op jit(solution)/shard_map/ppermute | solution.py:223
  41.8 7.8 %collective-permute-start.11 = (bf16[96,128]{1,0:T(8,128)(2,1)S(1)}, bf16[96,128]{1,0:T(8,128)(2,1)S(1)}, u32[]{:S(2)}, u32[]{:S(2)}) collective-permute-start(bf16[96,128]{1,0:T(8,128)(2,1)S(1)} %get-tuple-element.60), channel_id=1, source_target_pairs={{0,8},{1,2},{2,1},{3,4},{4,3},{5,6},{6,5},{7,15},{8,0},{9,10},{10,... | collective-permute-start | bytes 73736 | tf_op jit(solution)/shard_map/ppermute | solution.py:223
  50.8 1.4 %collective-permute-start.15 = (bf16[4,48,192]{2,1,0:T(8,128)(2,1)S(1)}, bf16[4,48,192]{2,1,0:T(8,128)(2,1)S(1)}, u32[]{:S(2)}, u32[]{:S(2)}) collective-permute-start(bf16[4,48,192]{2,1,0:T(8,128)(2,1)S(1)} %fusion.1), channel_id=1, source_target_pairs={{0,1},{1,0},{2,3},{3,2},{4,5},{5,4},{6,7},{7,6},{8,9},{9,8},{10,11... | collective-permute-start | bytes 221192 | tf_op jit(solution)/shard_map/ppermute | solution.py:223
  52.8 5.7 %collective-permute-start.18 = (bf16[48,192]{1,0:T(8,128)(2,1)S(1)}, bf16[48,192]{1,0:T(8,128)(2,1)S(1)}, u32[]{:S(2)}, u32[]{:S(2)}) collective-permute-start(bf16[48,192]{1,0:T(8,128)(2,1)S(1)} %get-tuple-element.71), channel_id=1, source_target_pairs={{0,6},{1,7},{2,4},{3,5},{4,2},{5,3},{6,0},{7,1},{8,14},{9,15},{10,... | collective-permute-start | bytes 55304 | tf_op jit(solution)/shard_map/ppermute | solution.py:234
  53.3 5.2 %collective-permute-start.17 = (bf16[48,192]{1,0:T(8,128)(2,1)S(1)}, bf16[48,192]{1,0:T(8,128)(2,1)S(1)}, u32[]{:S(2)}, u32[]{:S(2)}) collective-permute-start(bf16[48,192]{1,0:T(8,128)(2,1)S(1)} %get-tuple-element.72), channel_id=1, source_target_pairs={{0,4},{1,5},{2,6},{3,7},{4,0},{5,1},{6,2},{7,3},{8,12},{9,13},{10,... | collective-permute-start | bytes 55304 | tf_op jit(solution)/shard_map/ppermute | solution.py:234
  53.8 5.3 %collective-permute-start.16 = (bf16[48,192]{1,0:T(8,128)(2,1)S(1)}, bf16[48,192]{1,0:T(8,128)(2,1)S(1)}, u32[]{:S(2)}, u32[]{:S(2)}) collective-permute-start(bf16[48,192]{1,0:T(8,128)(2,1)S(1)} %get-tuple-element.73), channel_id=1, source_target_pairs={{0,2},{1,3},{2,0},{3,1},{4,6},{5,7},{6,4},{7,5},{8,10},{9,11},{10,... | collective-permute-start | bytes 55304 | tf_op jit(solution)/shard_map/ppermute | solution.py:234

commit v2 on v0

v2 whole, which is shorter than its diff:
```python
import functools

import jax
import jax.numpy as jnp
from jax import lax
from jax.experimental import pallas as pl
from jax.experimental.pallas import tpu as pltpu
from jax.sharding import PartitionSpec as P


DEGREE = 4

spectrum_center = 3.0
spectrum_half = 3.5

BF16 = jnp.bfloat16
F32 = jnp.float32
SHAPE = jax.ShapeDtypeStruct


ODD, FIRST, LAST, GROUP, CHIP, OFFSET = range(6)


def call(body, outs, ins, flops, scratch=(), raw=()):
    where = [pl.BlockSpec(memory_space=pltpu.SMEM)]
    for i in range(1, len(ins)):
        where.append(pl.BlockSpec(memory_space=pltpu.HBM if i in raw else pltpu.VMEM))
    ins = [pltpu.with_memory_space_constraint(x, pltpu.HBM) if i in raw else x for i, x in enumerate(ins)]
    return pl.pallas_call(
        body,
        out_shape=outs,
        in_specs=where,
        out_specs=jax.tree.map(lambda _: pl.BlockSpec(memory_space=pltpu.VMEM), outs),
        scratch_shapes=list(scratch),
        compiler_params=pltpu.CompilerParams(vmem_limit_bytes=24 << 20),
        cost_estimate=pl.CostEstimate(flops=flops, bytes_accessed=4 << 20, transcendentals=0),
    )(*ins)


def mm(a, b):
    return jnp.dot(a, b, preferred_element_type=F32)


def mm_nt(a, b):
    return lax.dot_general(a, b, (((1,), (1,)), ((), ())), preferred_element_type=F32)


def sort_out(place, got_a, got_b):
    odd = place[ODD] == 1
    got_a, got_b = got_a.astype(F32), got_b.astype(F32)
    low = jnp.where(place[FIRST] == 1, 0.0, jnp.where(odd, got_a, got_b))
    high = jnp.where(place[LAST] == 1, 0.0, jnp.where(odd, got_b, got_a))
    return low, high


def hand_out(place, low, high, give_a_ref, give_b_ref):
    odd = place[ODD] == 1
    give_a_ref[...] = jnp.where(odd, low, high).astype(give_a_ref.dtype)
    give_b_ref[...] = jnp.where(odd, high, low).astype(give_b_ref.dtype)


def halo_body(place, states_ref, potential_ref, index_ref,
              give_a_ref, give_b_ref, local_ref, low_ref, high_ref, row_ref, sem):
    count, owned = states_ref.shape
    rim = low_ref.shape[1]
    copies = [
        pltpu.make_async_copy(states_ref.at[:, pl.ds(0, rim)], low_ref, sem.at[0]),
        pltpu.make_async_copy(states_ref.at[:, pl.ds(owned - rim, rim)], high_ref, sem.at[1]),
        pltpu.make_async_copy(potential_ref, row_ref, sem.at[2]),
        pltpu.make_async_copy(index_ref, local_ref, sem.at[3]),
    ]
    for copy in copies:
        copy.start()
    for copy in copies:
        copy.wait()
    odd = place[ODD] == 1
    low, high = low_ref[...].astype(F32), high_ref[...].astype(F32)
    give_a_ref[:count, :] = jnp.where(odd, low, high).astype(BF16)
    give_b_ref[:count, :] = jnp.where(odd, high, low).astype(BF16)
    for take, give_ref in ((odd, give_a_ref), (jnp.logical_not(odd), give_b_ref)):
        row = jnp.where(take, row_ref[:, :rim], row_ref[:, owned - rim :])
        row = jnp.broadcast_to(row, (16, rim))
        at = lax.broadcasted_iota(jnp.int32, row.shape, 0)
        first = row.astype(BF16).astype(F32)
        second = (row - first).astype(BF16).astype(F32)
        third = (row - first) - second
        give_ref[count:, :] = jnp.where(
            at == 0, first, jnp.where(at == 1, second, jnp.where(at == 2, third, 0.0))
        ).astype(BF16)


def spread_body(place, index_ref, cells_ref, hot_ref, wide_ref, cells, sem):
    copy = pltpu.make_async_copy(cells_ref, cells, sem)
    copy.start()
    number, nodes, _ = cells_ref.shape
    extent = hot_ref.shape[0]
    for c in range(number):
        index = index_ref[c : c + 1, :] - place[OFFSET]
        hot = lax.broadcasted_iota(jnp.int32, (extent, nodes), 0) == index
        hot_ref[:, c * nodes : (c + 1) * nodes] = hot.astype(BF16)
    copy.wait()
    for c in range(number):
        here = slice(c * nodes, (c + 1) * nodes)
        wide_ref[:, here] = mm(hot_ref[:, here], cells[c]).astype(BF16)


def first_zone_body(place, states_ref, halo_a_ref, halo_b_ref, potential_ref, hot_ref, wide_ref,
                    inner_ref, zone_ref, shift_inner_ref, shift_zone_ref, picked_ref, sums_ref, give_a_ref, give_b_ref):
    count, owned = states_ref.shape
    rim = halo_a_ref.shape[1]
    width, extent = 2 * rim, owned + 2 * rim
    low, high = sort_out(place, halo_a_ref[...], halo_b_ref[...])
    zone_ref[:, :rim] = low[:count].astype(BF16)
    zone_ref[:, rim:width] = states_ref[:, :rim]
    zone_ref[:, width : width + rim] = states_ref[:, owned - rim :]
    zone_ref[:, width + rim :] = high[:count].astype(BF16)
    inner_ref[...] = states_ref[:, rim : owned - rim]
    row = potential_ref[...] - spectrum_center
    shift_inner_ref[...] = row[:, rim : owned - rim]
    shift_zone_ref[:, rim:width] = row[:, :rim]
    shift_zone_ref[:, width : width + rim] = row[:, owned - rim :]
    for got, at in ((low, 0), (high, width + rim)):
        part = got[count : count + 8]
        shift_zone_ref[:, at : at + rim] = (part[0:1] + part[1:2] + part[2:3]) - spectrum_center
    picked = (
        mm(inner_ref[...], hot_ref[width : extent - width, :])
        + mm(zone_ref[:, :width], hot_ref[:width, :])
        + mm(zone_ref[:, width:], hot_ref[extent - width :, :])
    ).astype(BF16)
    picked_ref[...] = picked
    low, high = mm_nt(picked, wide_ref[:width, :]), mm_nt(picked, wide_ref[extent - width :, :])
    sums_ref[:, :width] = low
    sums_ref[:, width:] = high
    hand_out(place, low, high, give_a_ref, give_b_ref)


def first_inner_body(place, inner_ref, picked_ref, shift_inner_ref, hot_ref, wide_ref,
                     next_ref, matrix_ref, diagonal_ref, part_ref):
    extent = matrix_ref.shape[0]
    width = (extent - inner_ref.shape[1]) // 2
    inside = slice(width, extent - width)
    value = mm_nt(picked_ref[...], wide_ref[inside, :]) + shift_inner_ref[...] * inner_ref[...].astype(F32)
    following = (value * (1.0 / spectrum_half)).astype(BF16)
    next_ref[...] = following
    step = 256
    for start in range(0, extent, step):
        rows = mm_nt(wide_ref[start : start + step, :], hot_ref[...])
        same = lax.broadcasted_iota(jnp.int32, (step, step), 0) == lax.broadcasted_iota(
            jnp.int32, (step, step), 1
        )
        square = rows[:, start : start + step]
        diagonal_ref[:, start : start + step] = jnp.sum(
            jnp.where(same, square, 0.0), axis=0, keepdims=True
        )
        matrix_ref[start : start + step, :] = rows.astype(BF16)
        matrix_ref[start : start + step, start : start + step] = jnp.where(same, 0.0, square).astype(BF16)
    part_ref[...] = mm(following, matrix_ref[inside, :])


def close_zones(place, sums_ref, got_a_ref, got_b_ref, shift_zone_ref, mid_ref, old_ref, scale, zone_ref):
    width = got_a_ref.shape[1]
    low, high = sort_out(place, got_a_ref[...], got_b_ref[...])
    for got, here in ((low, slice(0, width)), (high, slice(width, 2 * width))):
        value = sums_ref[:, here] + got + shift_zone_ref[:, here] * mid_ref[:, here].astype(F32)
        value = value * scale
        if old_ref is not None:
            value = value - old_ref[:, here].astype(F32)
        zone_ref[:, here] = value.astype(BF16)


def zone_sums(zone_ref, part_ref, matrix_ref, diagonal_ref):
    extent = matrix_ref.shape[0]
    width = zone_ref.shape[1] // 2
    low, high = zone_ref[:, :width], zone_ref[:, width:]
    out = []
    for here, own in ((slice(0, width), low), (slice(extent - width, extent), high)):
        out.append(
            part_ref[:, here]
            + mm(low, matrix_ref[:width, here])
            + mm(high, matrix_ref[extent - width :, here])
            + diagonal_ref[:, here] * own.astype(F32)
        )
    return out


def zone_body(has_old, scale, place, sums_ref, got_a_ref, got_b_ref, shift_zone_ref, mid_ref, *rest):
    old_ref, rest = (rest[0], rest[1:]) if has_old else (None, rest)
    part_ref, matrix_ref, diagonal_ref, zone_ref, next_sums_ref, give_a_ref, give_b_ref = rest
    close_zones(place, sums_ref, got_a_ref, got_b_ref, shift_zone_ref, mid_ref, old_ref, scale, zone_ref)
    low, high = zone_sums(zone_ref, part_ref, matrix_ref, diagonal_ref)
    width = low.shape[1]
    next_sums_ref[:, :width] = low
    next_sums_ref[:, width:] = high
    hand_out(place, low, high, give_a_ref, give_b_ref)


def inner_sums(zone_ref, inner_ref, part_ref, matrix_ref, diagonal_ref):
    extent = matrix_ref.shape[0]
    width = zone_ref.shape[1] // 2
    inside = slice(width, extent - width)
    return (
        part_ref[:, inside]
        + mm(zone_ref[:, :width], matrix_ref[:width, inside])
        + mm(zone_ref[:, width:], matrix_ref[extent - width :, inside])
        + diagonal_ref[:, inside] * inner_ref[...].astype(F32)
    )


def inner_body(place, zone_ref, inner_ref, old_ref, part_ref, shift_inner_ref, matrix_ref, diagonal_ref,
               next_ref, *next_part):
    sums = inner_sums(zone_ref, inner_ref, part_ref, matrix_ref, diagonal_ref)
    value = (sums + shift_inner_ref[...] * inner_ref[...].astype(F32)) * (2.0 / spectrum_half)
    following = (value - old_ref[...].astype(F32)).astype(BF16)
    next_ref[...] = following
    if next_part:
        part_body(place, next_ref, matrix_ref, *next_part)


def part_body(place, inner_ref, matrix_ref, part_ref):
    extent = matrix_ref.shape[0]
    width = (extent - inner_ref.shape[1]) // 2
    part_ref[...] = mm(inner_ref[...], matrix_ref[width : extent - width, :])


def energy_zone_body(place, sums_ref, got_a_ref, got_b_ref, shift_zone_ref, mid_ref, old_ref,
                     part_ref, matrix_ref, diagonal_ref, zone_ref, rim_ref, energy_ref, give_a_ref, give_b_ref):
    close_zones(place, sums_ref, got_a_ref, got_b_ref, shift_zone_ref, mid_ref, old_ref,
                2.0 / spectrum_half, zone_ref)
    width = got_a_ref.shape[1]
    rim = width // 2
    rim_ref[...] = zone_ref[:, rim : width + rim]
    low, high = zone_sums(zone_ref, part_ref, matrix_ref, diagonal_ref)
    own = shift_zone_ref[:, rim : width + rim] + spectrum_center
    own = own * rim_ref[...].astype(F32)
    energy_ref[:, :rim] = low[:, rim:] + own[:, :rim]
    energy_ref[:, rim:] = high[:, :rim] + own[:, rim:]
    hand_out(place, low[:, :rim], high[:, rim:], give_a_ref, give_b_ref)


def energy_inner_body(place, zone_ref, inner_ref, part_ref, shift_inner_ref, matrix_ref, diagonal_ref,
                      energy_ref, filtered_ref):
    sums = inner_sums(zone_ref, inner_ref, part_ref, matrix_ref, diagonal_ref)
    own = (shift_inner_ref[...] + spectrum_center) * inner_ref[...].astype(F32)
    energy_ref[...] = (sums + own).astype(BF16)
    width = zone_ref.shape[1] // 2
    rim = width // 2
    owned = filtered_ref.shape[1]
    filtered_ref[:, :rim] = zone_ref[:, rim:width]
    filtered_ref[:, rim : owned - rim] = inner_ref[...]
    filtered_ref[:, owned - rim :] = zone_ref[:, width : width + rim]


def project_body(scale, place, energy_rim_ref, got_a_ref, got_b_ref, energy_inner_ref, *refs):
    *blocks, out_ref, give_ref, stack_ref, pair_ref = refs
    count, inside = energy_inner_ref.shape
    rim = got_a_ref.shape[1]
    low, high = sort_out(place, got_a_ref[...], got_b_ref[...])
    group = place[GROUP]
    groups = len(blocks) // 2
    for distance in range(groups):
        inner_ref, rim_ref = blocks[2 * distance : 2 * distance + 2]
        at = pl.multiple_of((group ^ distance) * count, count)
        stack_ref[pl.ds(at, count), :inside] = inner_ref[...]
        stack_ref[pl.ds(at, count), inside:] = rim_ref[...]
    pair_ref[:count, :inside] = blocks[0][...]
    pair_ref[:count, inside:] = blocks[1][...]
    pair_ref[count:, :inside] = energy_inner_ref[...]
    pair_ref[count:, inside : inside + rim] = (energy_rim_ref[:, :rim] + low).astype(BF16)
    pair_ref[count:, inside + rim :] = (energy_rim_ref[:, rim:] + high).astype(BF16)
    both = mm_nt(stack_ref[...], pair_ref[...]) * scale
    chips, _, columns, _ = out_ref.shape
    odd = place[ODD] == 1
    for chip in range(chips):
        parts = [both[(2 * chip + core) * columns : (2 * chip + core + 1) * columns] for core in range(2)]
        for core in range(2):
            out_ref[chip, core] = parts[core].astype(BF16)
        give_ref[chip] = jnp.where(odd, parts[0], parts[1]).astype(BF16)


def halve_body(place, mine_ref, got_ref, *pieces):
    for distance, piece_ref in enumerate(pieces):
        chip = place[CHIP] ^ distance
        total = mine_ref[chip, place[ODD]].astype(F32) + got_ref[chip].astype(F32)
        piece_ref[...] = total.astype(BF16)


def final_body(count, place, *refs):
    parts, (first_ref, second_ref) = refs[:-2], refs[-2:]
    total = parts[0][...].astype(F32)
    for part in parts[1:]:
        total = total + part[...].astype(F32)
    first_ref[...] = total[:, :count]
    second_ref[...] = total[:, count:]


def swap(block, n_state, n_space, lead):
    route = []
    for s in range(n_state):
        for i in range(n_space):
            j = i + 1 if (i - lead) % 2 == 0 else i - 1
            if 0 <= j < n_space:
                route.append((s * n_space + i, s * n_space + j))
            elif (s ^ 1) < n_state:
                route.append((s * n_space + i, (s ^ 1) * n_space + i))
    return lax.ppermute(block, ("state", "space"), route)


def exchange(give_a, give_b, n_state, n_space):
    got_a = swap(give_a, n_state, n_space, 0)
    got_b = swap(give_b, n_state, n_space, 1)
    return got_a, got_b


def across(block, axis, distance):
    return lax.ppermute(block, axis, [(i, i ^ distance) for i in range(lax.axis_size(axis))])


def program(states_in, cell_matrices, connectivity, potential):
    count, owned = states_in.shape
    cells, nodes, _ = cell_matrices.shape
    rim = nodes // 4
    extent, inside = owned + 2 * rim, owned - 2 * rim
    n_state, n_space = lax.axis_size("state"), lax.axis_size("space")
    me = lax.axis_index("space")
    place = jnp.stack(
        [
            me & 1,
            (me == 0).astype(jnp.int32),
            (me == n_space - 1).astype(jnp.int32),
            lax.axis_index("state"),
            me >> 1,
            me * owned - rim,
        ]
    ).astype(jnp.int32)
    row = potential.reshape(1, owned)
    work = 2 * count * extent * extent
    inner, part = SHAPE((count, inside), BF16), SHAPE((count, extent), F32)
    zone, sums_of = SHAPE((count, 4 * rim), BF16), SHAPE((count, 4 * rim), F32)
    give, give_rim = SHAPE((count, 2 * rim), BF16), SHAPE((count, rim), BF16)

    halo = SHAPE((count + 16, rim), BF16)
    *gave, local = call(
        halo_body, (halo, halo, SHAPE(connectivity.shape, connectivity.dtype)),
        (place, states_in, row, connectivity), 0, raw=(1, 2, 3),
        scratch=[
            pltpu.VMEM((count, rim), BF16), pltpu.VMEM((count, rim), BF16),
            pltpu.VMEM((1, owned), F32), pltpu.SemaphoreType.DMA((4,)),
        ],
    )
    got = exchange(*gave, n_state, n_space)
    table = SHAPE((extent, cells * nodes), BF16)
    hot, wide = call(
        spread_body, (table, table), (place, local, cell_matrices),
        2 * extent * cells * nodes * nodes, raw=(2,),
        scratch=[pltpu.VMEM(cell_matrices.shape, BF16), pltpu.SemaphoreType.DMA],
    )
    inner_0, zone_0, shift_inner, shift_zone, picked, sums, *gave = call(
        first_zone_body,
        (inner, zone, SHAPE((1, inside), F32), SHAPE((1, 4 * rim), F32),
         SHAPE((count, cells * nodes), BF16), sums_of, give, give),
        (place, states_in, *got, row, hot, wide), work,
    )
    got = exchange(*gave, n_state, n_space)
    inner_1, matrix, diagonal, partial = call(
        first_inner_body,
        (inner, SHAPE((extent, extent), BF16), SHAPE((1, extent), F32), part),
        (place, inner_0, picked, shift_inner, hot, wide), 2 * extent * extent * cells * nodes,
    )
    inners, zones = [inner_0, inner_1], [zone_0]
    for k in range(1, DEGREE):
        older = zones[-2:-1]
        scale = (2.0 if older else 1.0) / spectrum_half
        zone_k, sums, *gave = call(
            functools.partial(zone_body, bool(older), scale),
            (zone, sums_of, give, give),
            (place, sums, *got, shift_zone, zones[-1], *older, partial, matrix, diagonal), work // 6,
        )
        zones.append(zone_k)
        got = exchange(*gave, n_state, n_space)
        ins = (place, zone_k, inners[-1], inners[-2], partial, shift_inner, matrix, diagonal)
        if k < DEGREE - 1:
            inner_k, partial = call(inner_body, (inner, part), ins, work)
        else:
            inner_k = call(inner_body, inner, ins, work // 4)
            partial = call(part_body, part, (place, inner_k, matrix), work // 2)
        inners.append(inner_k)
    distances = range(1, n_state)
    blocks = [inner_k] + [across(inner_k, "state", d) for d in distances]
    zone_k, rims, energy_rim, *gave = call(
        energy_zone_body,
        (zone, give, SHAPE((count, 2 * rim), F32), give_rim, give_rim),
        (place, sums, *got, shift_zone, zones[-1], zones[-2], partial, matrix, diagonal), work // 6,
    )
    rim_blocks = [rims] + [across(rims, "state", d) for d in distances]
    got = exchange(*gave, n_state, n_space)
    energy_inner, filtered = call(
        energy_inner_body, (inner, SHAPE((count, owned), BF16)),
        (place, zone_k, inner_k, partial, shift_inner, matrix, diagonal), work // 4,
    )
    total_states = count * n_state
    columns = total_states // n_space
    chips = n_space // 2
    mine, give_half = call(
        functools.partial(project_body, 1.0 / (owned * n_space)),
        (SHAPE((chips, 2, columns, 2 * count), BF16), SHAPE((chips, columns, 2 * count), BF16)),
        (place, energy_rim, *got, energy_inner, *(b for pair in zip(blocks, rim_blocks) for b in pair)),
        4 * total_states * count * owned,
        scratch=[pltpu.VMEM((total_states, owned), BF16), pltpu.VMEM((2 * count, owned), BF16)],
    )
    got_half = swap(give_half, n_state, n_space, 0)
    piece = SHAPE((columns, 2 * count), BF16)
    pieces = call(halve_body, (piece,) * chips, (place, mine, got_half), 0)
    pieces = [pieces[0]] + [across(p, "space", 2 * d) for d, p in enumerate(pieces) if d]
    turned = SHAPE((columns, count), F32)
    intersection, projected = call(
        functools.partial(final_body, count), (turned, turned), (place, *pieces), 0
    )
    return filtered, intersection.T, projected.T


def solution(mesh):
    return jax.shard_map(
        program,
        mesh=mesh,
        in_specs=(P("state", "space"), P("space", None, None), P("space", None), P("space")),
        out_specs=(P("state", "space"), P("state", "space"), P("state", "space")),
        check_vma=False,
    )
```

time: 223 us -> 58.6 us (0.26)
  waiting for transfers between devices: 76.2 us -> 12.9 us
  other arithmetic: 38.9 us -> 0 us
  starting transfers between devices: 56 us -> 22 us
  Pallas kernels: 0 us -> 22.6 us
  local copies, waits for them, and re-layouts: 20.2 us -> 0.1 us
  between operations: 14.8 us -> 0.85 us
  blocking collectives: 12.1 us -> 0 us
  matrix products: 4.05 us -> 0 us
    reduce_scatter x2 -> x0, waiting for transfers between devices: 57.8 us -> none  [the longest x1 29.7 us: per_device(): lax.psum_scatter(projected.astype(jnp.bfloat16), 'space', scatter_dimensi...]
    scatter-add x15 -> x0, other arithmetic: 34.3 us -> none  [the longest x5 30.9 us: apply_hamiltonian(): summed.at[:, local_index.reshape(-1)]]
    ppermute x20 -> x22, starting transfers between devices: 56 us -> 22 us  [the longest x9 11 us: across(): lax.ppermute(block, axis, [(i, i ^ distance) for i in range(lax.axis_size...]
    pallas_call x0 -> x16, Pallas kernels: none -> 22.6 us  [call(): pl.pallas_call(body, out_shape=outs, in_specs=where, out_specs=jax.tree.m...]
    gather x10 -> x0, local copies, waits for them, and re-layouts: 16.7 us -> none  [apply_hamiltonian(): picked = extended[:, local_index]]
    all_gather x1 -> x0, blocking collectives: 12.1 us -> none  [per_device(): incoming = lax.all_gather(current, 'state', axis=0, tiled=True)]
    ppermute x20 -> x22, waiting for transfers between devices: 18.3 us -> 12.9 us  [the longest x13 7.48 us: swap(): return lax.ppermute(block, ('state', 'space'), route)]
    dot_general x7 -> x0, matrix products: 4.05 us -> none  [the longest x1 1.54 us: per_device(): lax.dot_general(energy, incoming.astype(jnp.float32), contract, precision...]
  transfers between devices with their start and end apart: 22 -> 22, of which waited for: 11 -> 9; matrix products, arithmetic and copies ran while one was open for 2% -> 0% of each run, Pallas kernels for 0% -> 25%
where the time goes in v2:
time: 58.6 us; the launch traced here: 58.4 us
  Pallas kernels  22.6 us (39%)
  starting transfers between devices  22 us (38%)
  waiting for transfers between devices  12.9 us (22%)
  between operations  0.85 us (1%)
    pallas_call x16, Pallas kernels, call(): pl.pallas_call(body, out_shape=outs, in_specs=where, out_specs=jax.tree.m...  22.6 us
    ppermute x9, starting transfers between devices, across(): lax.ppermute(block, axis, [(i, i ^ distance) for i in range(lax.axis_size...  11 us
    ppermute x13, starting transfers between devices, swap(): return lax.ppermute(block, ('state', 'space'), route)  11 us
    ppermute x13, waiting for transfers between devices, swap(): return lax.ppermute(block, ('state', 'space'), route)  7.48 us
    ppermute x9, waiting for transfers between devices, across(): lax.ppermute(block, axis, [(i, i ^ distance) for i in range(lax.axis_size...  5.37 us
  transfers between devices with their start and end apart: 22, of which 9 were waited for; matrix products, arithmetic and copies ran while one was open for 0% of the time, Pallas kernels for 25%

profile of v2, /device:TPU:0, one launch (start us, length us, event | category | flops | bytes accessed | tf_op | source)
XLA Modules:
  0.0 58.4 jit_solution(7225004432185619871)
XLA Ops:
  0.7 1.4 %shard_map.67 = (bf16[112,128]{1,0:T(8,128)(2,1)S(1)}, bf16[112,128]{1,0:T(8,128)(2,1)S(1)}, s32[2,512]{1,0:T(2,128)S(1)}) custom-call(s32[6]{0:T(128)S(1)} %stack.35.place, bf16[96,1024]{1,0:T(8,128)(2,1)} %states_ref.3, f32[1,1024]{1,0:T(1,128)} %bitcast.9, s32[2,512]{1,0:T(2,128)} %index_ref.1), custom_call_target="tpu_custom_call" | custom-call | bytes 4194304 | tf_op jit(solution)/shard_map/pallas_call | solution.py:29
  2.7 2.6 %collective-permute-start.1 = (bf16[112,128]{1,0:T(8,128)(2,1)S(1)}, bf16[112,128]{1,0:T(8,128)(2,1)S(1)}, u32[]{:S(2)}, u32[]{:S(2)}) collective-permute-start(bf16[112,128]{1,0:T(8,128)(2,1)S(1)} %get-tuple-element.52), channel_id=1, source_target_pairs={{0,8},{1,2},{2,1},{3,4},{4,3},{5,6},{6,5},{7,15},{8,0},{9,10},{10,... | collective-permute-start | bytes 86024 | tf_op jit(solution)/shard_map/ppermute | solution.py:305
  5.2 3.3 %shard_map.68 = (bf16[1280,1024]{1,0:T(8,128)(2,1)S(1)}, bf16[1280,1024]{1,0:T(8,128)(2,1)S(1)}) custom-call(s32[6]{0:T(128)S(1)} %stack.35.place, s32[2,512]{1,0:T(2,128)S(1)} %get-tuple-element.53.index_ref, bf16[2,512,512]{2,1,0:T(8,128)(2,1)} %cells_ref.1), custom_call_target="tpu_custom_call" | custom-call | flops 1342177280 | bytes 4194304 | tf_op jit(solution)/shard_map/pallas_call | solution.py:29
  8.6 1.4 %shard_map.69 = (bf16[96,768]{1,0:T(8,128)(2,1)S(1)}, bf16[96,512]{1,0:T(8,128)(2,1)S(1)}, f32[1,768]{1,0:T(1,128)S(1)}, f32[1,512]{1,0:T(1,128)S(1)}, bf16[96,1...) custom-call(s32[6]{0:T(128)S(1)} %stack.35.place, ...), custom_call_target="tpu_custom_call" | custom-call | flops 314572800 | bytes 4194304 | tf_op jit(solution)/shard_map/pallas_call | solution.py:29
  10.3 1.5 %collective-permute-start.3 = (bf16[96,256]{1,0:T(8,128)(2,1)S(1)}, bf16[96,256]{1,0:T(8,128)(2,1)S(1)}, u32[]{:S(2)}, u32[]{:S(2)}) collective-permute-start(bf16[96,256]{1,0:T(8,128)(2,1)S(1)} %get-tuple-element.58), channel_id=1, source_target_pairs={{0,8},{1,2},{2,1},{3,4},{4,3},{5,6},{6,5},{7,15},{8,0},{9,10},{10,... | collective-permute-start | bytes 147464 | tf_op jit(solution)/shard_map/ppermute | solution.py:305
  11.8 4.9 %shard_map.70 = (bf16[96,768]{1,0:T(8,128)(2,1)S(1)}, bf16[1280,1280]{1,0:T(8,128)(2,1)S(1)}, f32[1,1280]{1,0:T(1,128)S(1)}, f32[96,1280]{1,0:T(8,128)S(1)}) custom-call(s32[6]{0:T(128)S(1)} %stack.35.place, bf16[96,768]{1,0:T(8,128)(2,1)S(1)} %get-tuple-element.61.inner_ref.old_ref, bf16[96,1024]{1,0:T(8,128)(2,1)S(1)} %get-tuple-element.62.picked_ref, ...), custom_call_target="tpu_custom_call" | custom-call | flops 3355443200 | bytes 4194304 | tf_op jit(solution)/shard_map/pallas_call | solution.py:29
  17.8 1.5 %collective-permute-start.5 = (bf16[96,256]{1,0:T(8,128)(2,1)S(1)}, bf16[96,256]{1,0:T(8,128)(2,1)S(1)}, u32[]{:S(2)}, u32[]{:S(2)}) collective-permute-start(bf16[96,256]{1,0:T(8,128)(2,1)S(1)} %get-tuple-element.69), channel_id=1, source_target_pairs={{0,8},{1,2},{2,1},{3,4},{4,3},{5,6},{6,5},{7,15},{8,0},{9,10},{10,... | collective-permute-start | bytes 147464 | tf_op jit(solution)/shard_map/ppermute | solution.py:305
  19.2 1.2 %shard_map.72 = (bf16[96,768]{1,0:T(8,128)(2,1)S(1)}, f32[96,1280]{1,0:T(8,128)S(1)}) custom-call(s32[6]{0:T(128)S(1)} %stack.35.place, bf16[96,512]{1,0:T(8,128)(2,1)S(1)} %get-tuple-element.70.zone_ref.mid_ref.rest_0_, bf16[96,768]{1,0:T(8,128)(2,1)S(1)} %get-tuple-element.71.inner_ref.old_ref, bf16[96,768]{1,0:T(8,128)(2,1)S(1)} %get-tuple-element.61.inner_ref.old_ref, ...), custom_call_target="tpu_custom_call" | custom-call | flops 314572800 | bytes 4194304 | tf_op jit(solution)/shard_map/pallas_call | solution.py:29
  20.5 1.3 %collective-permute-done.5.got_b_ref = bf16[96,256]{1,0:T(8,128)(2,1)S(1)} collective-permute-done((bf16[96,256]{1,0:T(8,128)(2,1)S(1)}, bf16[96,256]{1,0:T(8,128)(2,1)S(1)}, u32[]{:S(2)}, u32[]{:S(2)}) %collective-permute-start.5) | collective-permute-done | bytes 49184 | tf_op jit(solution)/shard_map/ppermute | solution.py:305
  22.7 1.5 %collective-permute-start.7 = (bf16[96,256]{1,0:T(8,128)(2,1)S(1)}, bf16[96,256]{1,0:T(8,128)(2,1)S(1)}, u32[]{:S(2)}, u32[]{:S(2)}) collective-permute-start(bf16[96,256]{1,0:T(8,128)(2,1)S(1)} %get-tuple-element.75), channel_id=1, source_target_pairs={{0,8},{1,2},{2,1},{3,4},{4,3},{5,6},{6,5},{7,15},{8,0},{9,10},{10,... | collective-permute-start | bytes 147464 | tf_op jit(solution)/shard_map/ppermute | solution.py:305
  24.3 1.2 %shard_map.74 = (bf16[96,768]{1,0:T(8,128)(2,1)S(1)}, f32[96,1280]{1,0:T(8,128)S(1)}) custom-call(s32[6]{0:T(128)S(1)} %stack.35.place, bf16[96,512]{1,0:T(8,128)(2,1)S(1)} %get-tuple-element.76.zone_ref.mid_ref.old_ref, bf16[96,768]{1,0:T(8,128)(2,1)S(1)} %get-tuple-element.77.inner_ref.old_ref, bf16[96,768]{1,0:T(8,128)(2,1)S(1)} %get-tuple-element.71.inner_ref.old_ref, ...), custom_call_target="tpu_custom_call" | custom-call | flops 314572800 | bytes 4194304 | tf_op jit(solution)/shard_map/pallas_call | solution.py:29
  25.5 1.3 %collective-permute-done.7.got_b_ref = bf16[96,256]{1,0:T(8,128)(2,1)S(1)} collective-permute-done((bf16[96,256]{1,0:T(8,128)(2,1)S(1)}, bf16[96,256]{1,0:T(8,128)(2,1)S(1)}, u32[]{:S(2)}, u32[]{:S(2)}) %collective-permute-start.7) | collective-permute-done | bytes 49184 | tf_op jit(solution)/shard_map/ppermute | solution.py:305
  27.8 1.5 %collective-permute-start.9 = (bf16[96,256]{1,0:T(8,128)(2,1)S(1)}, bf16[96,256]{1,0:T(8,128)(2,1)S(1)}, u32[]{:S(2)}, u32[]{:S(2)}) collective-permute-start(bf16[96,256]{1,0:T(8,128)(2,1)S(1)} %get-tuple-element.81), channel_id=1, source_target_pairs={{0,8},{1,2},{2,1},{3,4},{4,3},{5,6},{6,5},{7,15},{8,0},{9,10},{10,... | collective-permute-start | bytes 147464 | tf_op jit(solution)/shard_map/ppermute | solution.py:305
  30.8 1.5 %collective-permute-start.14 = (bf16[96,768]{1,0:T(8,128)(2,1)S(1)}, bf16[96,768]{1,0:T(8,128)(2,1)S(1)}, u32[]{:S(2)}, u32[]{:S(2)}) collective-permute-start(bf16[96,768]{1,0:T(8,128)(2,1)S(1)} %shard_map.76.inner_ref.refs_0_), channel_id=1, source_target_pairs={{0,16},{8,24},{16,0},{24,8},{1,17},{9,25},{17,1},{25,9},{2,18},{10... | collective-permute-start | bytes 442376 | tf_op jit(solution)/shard_map/ppermute | solution.py:315
  32.3 1.4 %collective-permute-start.16 = (bf16[96,768]{1,0:T(8,128)(2,1)S(1)}, bf16[96,768]{1,0:T(8,128)(2,1)S(1)}, u32[]{:S(2)}, u32[]{:S(2)}) collective-permute-start(bf16[96,768]{1,0:T(8,128)(2,1)S(1)} %shard_map.76.inner_ref.refs_0_), channel_id=1, source_target_pairs={{0,24},{8,16},{16,8},{24,0},{1,25},{9,17},{17,9},{25,1},{2,26},{10... | collective-permute-start | bytes 442376 | tf_op jit(solution)/shard_map/ppermute | solution.py:315
  37.7 2.9 %collective-permute-done.11.got_b_ref = bf16[96,128]{1,0:T(8,128)(2,1)S(1)} collective-permute-done((bf16[96,128]{1,0:T(8,128)(2,1)S(1)}, bf16[96,128]{1,0:T(8,128)(2,1)S(1)}, u32[]{:S(2)}, u32[]{:S(2)}) %collective-permute-start.11) | collective-permute-done | bytes 24608 | tf_op jit(solution)/shard_map/ppermute | solution.py:305
  40.6 1.5 %collective-permute-start.15 = (bf16[96,256]{1,0:T(8,128)(2,1)S(1)}, bf16[96,256]{1,0:T(8,128)(2,1)S(1)}, u32[]{:S(2)}, u32[]{:S(2)}) collective-permute-start(bf16[96,256]{1,0:T(8,128)(2,1)S(1)} %get-tuple-element.90.refs_1_), channel_id=1, source_target_pairs={{0,16},{8,24},{16,0},{24,8},{1,17},{9,25},{17,1},{25,9},{2,18},{10... | collective-permute-start | bytes 147464 | tf_op jit(solution)/shard_map/ppermute | solution.py:315
  43.0 1.4 %shard_map.79 = (bf16[96,768]{1,0:T(8,128)(2,1)S(1)}, bf16[96,1024]{1,0:T(8,128)(2,1)}) custom-call(s32[6]{0:T(128)S(1)} %stack.35.place, bf16[96,512]{1,0:T(8,128)(2,1)S(1)} %get-tuple-element.84.zone_ref, bf16[96,768]{1,0:T(8,128)(2,1)S(1)} %shard_map.76.inner_ref.refs_0_, f32[96,1280]{1,0:T(8,128)S(1)} %shard_map.77.part_ref, ...), custom_call_target="tpu_custom_call" | custom-call | flops 78643200 | bytes 4194304 | tf_op jit(solution)/shard_map/pallas_call | solution.py:29
  44.7 2.4 %collective-permute-done.17.refs_7_ = bf16[96,256]{1,0:T(8,128)(2,1)S(1)} collective-permute-done((bf16[96,256]{1,0:T(8,128)(2,1)S(1)}, bf16[96,256]{1,0:T(8,128)(2,1)S(1)}, u32[]{:S(2)}, u32[]{:S(2)}) %collective-permute-start.17) | collective-permute-done | bytes 49184 | tf_op jit(solution)/shard_map/ppermute | solution.py:315
  48.2 1.3 %collective-permute-done.18.got_ref = bf16[4,48,192]{2,1,0:T(8,128)(2,1)S(1)} collective-permute-done((bf16[4,48,192]{2,1,0:T(8,128)(2,1)S(1)}, bf16[4,48,192]{2,1,0:T(8,128)(2,1)S(1)}, u32[]{:S(2)}, u32[]{:S(2)}) %collective-permute-start.18) | collective-permute-done | bytes 73760 | tf_op jit(solution)/shard_map/ppermute | solution.py:305
  50.4 1.1 %collective-permute-start.20 = (bf16[48,192]{1,0:T(8,128)(2,1)S(1)}, bf16[48,192]{1,0:T(8,128)(2,1)S(1)}, u32[]{:S(2)}, u32[]{:S(2)}) collective-permute-start(bf16[48,192]{1,0:T(8,128)(2,1)S(1)} %get-tuple-element.95), channel_id=1, source_target_pairs={{0,4},{1,5},{2,6},{3,7},{4,0},{5,1},{6,2},{7,3},{8,12},{9,13},{10,... | collective-permute-start | bytes 55304 | tf_op jit(solution)/shard_map/ppermute | solution.py:315
  51.5 3.0 %collective-permute-start.21 = (bf16[48,192]{1,0:T(8,128)(2,1)S(1)}, bf16[48,192]{1,0:T(8,128)(2,1)S(1)}, u32[]{:S(2)}, u32[]{:S(2)}) collective-permute-start(bf16[48,192]{1,0:T(8,128)(2,1)S(1)} %get-tuple-element.96), channel_id=1, source_target_pairs={{0,6},{1,7},{2,4},{3,5},{4,2},{5,3},{6,0},{7,1},{8,14},{9,15},{10,... | collective-permute-start | bytes 55304 | tf_op jit(solution)/shard_map/ppermute | solution.py:315
  55.4 1.7 %collective-permute-done.21.refs_3_ = bf16[48,192]{1,0:T(8,128)(2,1)S(1)} collective-permute-done((bf16[48,192]{1,0:T(8,128)(2,1)S(1)}, bf16[48,192]{1,0:T(8,128)(2,1)S(1)}, u32[]{:S(2)}, u32[]{:S(2)}) %collective-permute-start.21) | collective-permute-done | bytes 18464 | tf_op jit(solution)/shard_map/ppermute | solution.py:315
  57.1 1.2 %shard_map.82 = (f32[48,96]{1,0:T(8,128)}, f32[48,96]{1,0:T(8,128)}) custom-call(s32[6]{0:T(128)S(1)} %stack.35.place, bf16[48,192]{1,0:T(8,128)(2,1)S(1)} %get-tuple-element.93.refs_0_, bf16[48,192]{1,0:T(8,128)(2,1)S(1)} %collective-permute-done.19.refs_1_, bf16[48,192]{1,0:T(8,128)(2,1)S(1)} %collective-permute-done.20.refs_2_, ...), custom_call_target="tpu_custom_call" | custom-call | bytes 4194304 | tf_op jit(solution)/shard_map/pallas_call | solution.py:29
  (41 shorter events, 13.3 us)
Async XLA Ops:
  0.6 7.9 %copy-start = (bf16[96,1024]{1,0:T(8,128)(2,1)S(1)}, bf16[96,1024]{1,0:T(8,128)(2,1)}, u32[]{:S(2)}) copy-start(bf16[96,1024]{1,0:T(8,128)(2,1)} %states_ref.3) | copy-start | bytes 589828
  0.6 7.9 %copy-start.1 = (f32[1024]{0:T(1024)S(1)}, f32[1024]{0:T(1024)}, u32[]{:S(2)}) copy-start(f32[1024]{0:T(1024)} %param.7) | copy-start | bytes 12292
  2.1 6.4 %collective-permute-start = (bf16[112,128]{1,0:T(8,128)(2,1)S(1)}, bf16[112,128]{1,0:T(8,128)(2,1)S(1)}, u32[]{:S(2)}, u32[]{:S(2)}) collective-permute-start(bf16[112,128]{1,0:T(8,128)(2,1)S(1)} %get-tuple-element.51), channel_id=1, source_target_pairs={{0,1},{1,0},{2,3},{3,2},{4,5},{5,4},{6,7},{7,6},{8,9},{9,8},{10,11... | collective-permute-start | bytes 86024 | tf_op jit(solution)/shard_map/ppermute | solution.py:305
  2.7 5.9 %collective-permute-start.1 = (bf16[112,128]{1,0:T(8,128)(2,1)S(1)}, bf16[112,128]{1,0:T(8,128)(2,1)S(1)}, u32[]{:S(2)}, u32[]{:S(2)}) collective-permute-start(bf16[112,128]{1,0:T(8,128)(2,1)S(1)} %get-tuple-element.52), channel_id=1, source_target_pairs={{0,8},{1,2},{2,1},{3,4},{4,3},{5,6},{6,5},{7,15},{8,0},{9,10},{10,... | collective-permute-start | bytes 86024 | tf_op jit(solution)/shard_map/ppermute | solution.py:305
  10.0 6.7 %collective-permute-start.2 = (bf16[96,256]{1,0:T(8,128)(2,1)S(1)}, bf16[96,256]{1,0:T(8,128)(2,1)S(1)}, u32[]{:S(2)}, u32[]{:S(2)}) collective-permute-start(bf16[96,256]{1,0:T(8,128)(2,1)S(1)} %get-tuple-element.57), channel_id=1, source_target_pairs={{0,1},{1,0},{2,3},{3,2},{4,5},{5,4},{6,7},{7,6},{8,9},{9,8},{10,11... | collective-permute-start | bytes 147464 | tf_op jit(solution)/shard_map/ppermute | solution.py:305
  10.3 6.4 %collective-permute-start.3 = (bf16[96,256]{1,0:T(8,128)(2,1)S(1)}, bf16[96,256]{1,0:T(8,128)(2,1)S(1)}, u32[]{:S(2)}, u32[]{:S(2)}) collective-permute-start(bf16[96,256]{1,0:T(8,128)(2,1)S(1)} %get-tuple-element.58), channel_id=1, source_target_pairs={{0,8},{1,2},{2,1},{3,4},{4,3},{5,6},{6,5},{7,15},{8,0},{9,10},{10,... | collective-permute-start | bytes 147464 | tf_op jit(solution)/shard_map/ppermute | solution.py:305
  17.5 3.0 %collective-permute-start.4 = (bf16[96,256]{1,0:T(8,128)(2,1)S(1)}, bf16[96,256]{1,0:T(8,128)(2,1)S(1)}, u32[]{:S(2)}, u32[]{:S(2)}) collective-permute-start(bf16[96,256]{1,0:T(8,128)(2,1)S(1)} %get-tuple-element.68), channel_id=1, source_target_pairs={{0,1},{1,0},{2,3},{3,2},{4,5},{5,4},{6,7},{7,6},{8,9},{9,8},{10,11... | collective-permute-start | bytes 147464 | tf_op jit(solution)/shard_map/ppermute | solution.py:305
  17.8 4.1 %collective-permute-start.5 = (bf16[96,256]{1,0:T(8,128)(2,1)S(1)}, bf16[96,256]{1,0:T(8,128)(2,1)S(1)}, u32[]{:S(2)}, u32[]{:S(2)}) collective-permute-start(bf16[96,256]{1,0:T(8,128)(2,1)S(1)} %get-tuple-element.69), channel_id=1, source_target_pairs={{0,8},{1,2},{2,1},{3,4},{4,3},{5,6},{6,5},{7,15},{8,0},{9,10},{10,... | collective-permute-start | bytes 147464 | tf_op jit(solution)/shard_map/ppermute | solution.py:305
  22.6 2.9 %collective-permute-start.6 = (bf16[96,256]{1,0:T(8,128)(2,1)S(1)}, bf16[96,256]{1,0:T(8,128)(2,1)S(1)}, u32[]{:S(2)}, u32[]{:S(2)}) collective-permute-start(bf16[96,256]{1,0:T(8,128)(2,1)S(1)} %get-tuple-element.74), channel_id=1, source_target_pairs={{0,1},{1,0},{2,3},{3,2},{4,5},{5,4},{6,7},{7,6},{8,9},{9,8},{10,11... | collective-permute-start | bytes 147464 | tf_op jit(solution)/shard_map/ppermute | solution.py:305
  22.7 4.1 %collective-permute-start.7 = (bf16[96,256]{1,0:T(8,128)(2,1)S(1)}, bf16[96,256]{1,0:T(8,128)(2,1)S(1)}, u32[]{:S(2)}, u32[]{:S(2)}) collective-permute-start(bf16[96,256]{1,0:T(8,128)(2,1)S(1)} %get-tuple-element.75), channel_id=1, source_target_pairs={{0,8},{1,2},{2,1},{3,4},{4,3},{5,6},{6,5},{7,15},{8,0},{9,10},{10,... | collective-permute-start | bytes 147464 | tf_op jit(solution)/shard_map/ppermute | solution.py:305
  27.6 7.1 %collective-permute-start.8 = (bf16[96,256]{1,0:T(8,128)(2,1)S(1)}, bf16[96,256]{1,0:T(8,128)(2,1)S(1)}, u32[]{:S(2)}, u32[]{:S(2)}) collective-permute-start(bf16[96,256]{1,0:T(8,128)(2,1)S(1)} %get-tuple-element.80), channel_id=1, source_target_pairs={{0,1},{1,0},{2,3},{3,2},{4,5},{5,4},{6,7},{7,6},{8,9},{9,8},{10,11... | collective-permute-start | bytes 147464 | tf_op jit(solution)/shard_map/ppermute | solution.py:305
  27.8 6.9 %collective-permute-start.9 = (bf16[96,256]{1,0:T(8,128)(2,1)S(1)}, bf16[96,256]{1,0:T(8,128)(2,1)S(1)}, u32[]{:S(2)}, u32[]{:S(2)}) collective-permute-start(bf16[96,256]{1,0:T(8,128)(2,1)S(1)} %get-tuple-element.81), channel_id=1, source_target_pairs={{0,8},{1,2},{2,1},{3,4},{4,3},{5,6},{6,5},{7,15},{8,0},{9,10},{10,... | collective-permute-start | bytes 147464 | tf_op jit(solution)/shard_map/ppermute | solution.py:305
  30.2 17.0 %collective-permute-start.12 = (bf16[96,768]{1,0:T(8,128)(2,1)S(1)}, bf16[96,768]{1,0:T(8,128)(2,1)S(1)}, u32[]{:S(2)}, u32[]{:S(2)}) collective-permute-start(bf16[96,768]{1,0:T(8,128)(2,1)S(1)} %shard_map.76.inner_ref.refs_0_), channel_id=1, source_target_pairs={{0,8},{8,0},{16,24},{24,16},{1,9},{9,1},{17,25},{25,17},{2,10},{10... | collective-permute-start | bytes 442376 | tf_op jit(solution)/shard_map/ppermute | solution.py:315
  30.8 16.4 %collective-permute-start.14 = (bf16[96,768]{1,0:T(8,128)(2,1)S(1)}, bf16[96,768]{1,0:T(8,128)(2,1)S(1)}, u32[]{:S(2)}, u32[]{:S(2)}) collective-permute-start(bf16[96,768]{1,0:T(8,128)(2,1)S(1)} %shard_map.76.inner_ref.refs_0_), channel_id=1, source_target_pairs={{0,16},{8,24},{16,0},{24,8},{1,17},{9,25},{17,1},{25,9},{2,18},{10... | collective-permute-start | bytes 442376 | tf_op jit(solution)/shard_map/ppermute | solution.py:315
  32.3 14.9 %collective-permute-start.16 = (bf16[96,768]{1,0:T(8,128)(2,1)S(1)}, bf16[96,768]{1,0:T(8,128)(2,1)S(1)}, u32[]{:S(2)}, u32[]{:S(2)}) collective-permute-start(bf16[96,768]{1,0:T(8,128)(2,1)S(1)} %shard_map.76.inner_ref.refs_0_), channel_id=1, source_target_pairs={{0,24},{8,16},{16,8},{24,0},{1,25},{9,17},{17,9},{25,1},{2,26},{10... | collective-permute-start | bytes 442376 | tf_op jit(solution)/shard_map/ppermute | solution.py:315
  35.5 1.3 %collective-permute-start.10 = (bf16[96,128]{1,0:T(8,128)(2,1)S(1)}, bf16[96,128]{1,0:T(8,128)(2,1)S(1)}, u32[]{:S(2)}, u32[]{:S(2)}) collective-permute-start(bf16[96,128]{1,0:T(8,128)(2,1)S(1)} %get-tuple-element.87), channel_id=1, source_target_pairs={{0,1},{1,0},{2,3},{3,2},{4,5},{5,4},{6,7},{7,6},{8,9},{9,8},{10,11... | collective-permute-start | bytes 73736 | tf_op jit(solution)/shard_map/ppermute | solution.py:305
  35.6 6.5 %collective-permute-start.13 = (bf16[96,256]{1,0:T(8,128)(2,1)S(1)}, bf16[96,256]{1,0:T(8,128)(2,1)S(1)}, u32[]{:S(2)}, u32[]{:S(2)}) collective-permute-start(bf16[96,256]{1,0:T(8,128)(2,1)S(1)} %get-tuple-element.90.refs_1_), channel_id=1, source_target_pairs={{0,8},{8,0},{16,24},{24,16},{1,9},{9,1},{17,25},{25,17},{2,10},{10... | collective-permute-start | bytes 147464 | tf_op jit(solution)/shard_map/ppermute | solution.py:315
  36.8 3.8 %collective-permute-start.11 = (bf16[96,128]{1,0:T(8,128)(2,1)S(1)}, bf16[96,128]{1,0:T(8,128)(2,1)S(1)}, u32[]{:S(2)}, u32[]{:S(2)}) collective-permute-start(bf16[96,128]{1,0:T(8,128)(2,1)S(1)} %get-tuple-element.88), channel_id=1, source_target_pairs={{0,8},{1,2},{2,1},{3,4},{4,3},{5,6},{6,5},{7,15},{8,0},{9,10},{10,... | collective-permute-start | bytes 73736 | tf_op jit(solution)/shard_map/ppermute | solution.py:305
  40.6 4.1 %collective-permute-start.15 = (bf16[96,256]{1,0:T(8,128)(2,1)S(1)}, bf16[96,256]{1,0:T(8,128)(2,1)S(1)}, u32[]{:S(2)}, u32[]{:S(2)}) collective-permute-start(bf16[96,256]{1,0:T(8,128)(2,1)S(1)} %get-tuple-element.90.refs_1_), channel_id=1, source_target_pairs={{0,16},{8,24},{16,0},{24,8},{1,17},{9,25},{17,1},{25,9},{2,18},{10... | collective-permute-start | bytes 147464 | tf_op jit(solution)/shard_map/ppermute | solution.py:315
  42.1 5.0 %collective-permute-start.17 = (bf16[96,256]{1,0:T(8,128)(2,1)S(1)}, bf16[96,256]{1,0:T(8,128)(2,1)S(1)}, u32[]{:S(2)}, u32[]{:S(2)}) collective-permute-start(bf16[96,256]{1,0:T(8,128)(2,1)S(1)} %get-tuple-element.90.refs_1_), channel_id=1, source_target_pairs={{0,24},{8,16},{16,8},{24,0},{1,25},{9,17},{17,9},{25,1},{2,26},{10... | collective-permute-start | bytes 147464 | tf_op jit(solution)/shard_map/ppermute | solution.py:315
  48.1 1.4 %collective-permute-start.18 = (bf16[4,48,192]{2,1,0:T(8,128)(2,1)S(1)}, bf16[4,48,192]{2,1,0:T(8,128)(2,1)S(1)}, u32[]{:S(2)}, u32[]{:S(2)}) collective-permute-start(bf16[4,48,192]{2,1,0:T(8,128)(2,1)S(1)} %get-tuple-element.92), channel_id=1, source_target_pairs={{0,1},{1,0},{2,3},{3,2},{4,5},{5,4},{6,7},{7,6},{8,9},{9,8},{10,11... | collective-permute-start | bytes 221192 | tf_op jit(solution)/shard_map/ppermute | solution.py:305
  50.0 4.5 %collective-permute-start.19 = (bf16[48,192]{1,0:T(8,128)(2,1)S(1)}, bf16[48,192]{1,0:T(8,128)(2,1)S(1)}, u32[]{:S(2)}, u32[]{:S(2)}) collective-permute-start(bf16[48,192]{1,0:T(8,128)(2,1)S(1)} %get-tuple-element.94), channel_id=1, source_target_pairs={{0,2},{1,3},{2,0},{3,1},{4,6},{5,7},{6,4},{7,5},{8,10},{9,11},{10,... | collective-permute-start | bytes 55304 | tf_op jit(solution)/shard_map/ppermute | solution.py:315
  50.4 5.0 %collective-permute-start.20 = (bf16[48,192]{1,0:T(8,128)(2,1)S(1)}, bf16[48,192]{1,0:T(8,128)(2,1)S(1)}, u32[]{:S(2)}, u32[]{:S(2)}) collective-permute-start(bf16[48,192]{1,0:T(8,128)(2,1)S(1)} %get-tuple-element.95), channel_id=1, source_target_pairs={{0,4},{1,5},{2,6},{3,7},{4,0},{5,1},{6,2},{7,3},{8,12},{9,13},{10,... | collective-permute-start | bytes 55304 | tf_op jit(solution)/shard_map/ppermute | solution.py:315
  51.5 5.6 %collective-permute-start.21 = (bf16[48,192]{1,0:T(8,128)(2,1)S(1)}, bf16[48,192]{1,0:T(8,128)(2,1)S(1)}, u32[]{:S(2)}, u32[]{:S(2)}) collective-permute-start(bf16[48,192]{1,0:T(8,128)(2,1)S(1)} %get-tuple-element.96), channel_id=1, source_target_pairs={{0,6},{1,7},{2,4},{3,5},{4,2},{5,3},{6,0},{7,1},{8,14},{9,15},{10,... | collective-permute-start | bytes 55304 | tf_op jit(solution)/shard_map/ppermute | solution.py:315
